TPU v7x, 32 devices: a whole 2x2x4 slice. The times are simulated.
32 devices in a mesh: dp: 2 (over y), row: 4 (over x, core), col: 4 (over z).
Axes of the slice: x: 2, y: 2, z: 4, core: 2. Of those that a mesh axis runs over, the one named last changes fastest.
Arguments:
- inputs: bfloat16 [4096, 1024], P(('dp', 'row'), 'col'), may hold values from -6 to 6
- cotangent: bfloat16 [4096, 1024], P(('dp', 'row'), 'col'), may hold values from -6 to 6
- mixer_in: bfloat16 [1024, 4120], P('col', 'row'), may hold values from -0.1875 to 0.1875
- mixer_out: bfloat16 [2048, 1024], P('row', 'col'), may hold values from -0.1875 to 0.1875
- expand_weight: bfloat16 [1024, 4096], P('col', 'row'), may hold values from -0.1875 to 0.1875
- shrink_weight: bfloat16 [2048, 1024], P('row', 'col'), may hold values from -0.125 to 0.125
- input_gain: float32 [1024], P('col'), may hold values from 0.1 to 1.9
- middle_gain: float32 [1024], P('col'), may hold values from 0.1 to 1.9
- mixer_kernel: float32 [4, 1536], P(None, 'row'), may hold values from -3 to 3
- shared_kernel: float32 [4, 256], replicated, may hold values from -3 to 3
- decay_log: float32 [24], P('row'), may hold values from -4 to 0.5
- step_bias: float32 [24], P('row'), may hold values from -4 to -1
- skip_scale: float32 [24], P('row'), may hold values from 0.5 to 2
- state_gain: float32 [1536], P('row'), may hold values from 0.1 to 1.9
- dealing: int32 [4, 4, 2], replicated, may hold values from 0 to 1, as said below
- lengths: int32 [4, 2, 4, 4], replicated, may hold values from 1 to 96, 128 in all within a row
Outputs:
- outputs: bfloat16 [4096, 1024], P(('dp', 'row'), 'col')
- input_grad: bfloat16 [4096, 1024], P(('dp', 'row'), 'col')
- mixer_in_grad: float32 [1024, 4120], P('col', 'row')
- mixer_out_grad: float32 [2048, 1024], P('row', 'col')
- expand_grad: float32 [1024, 4096], P('col', 'row')
- shrink_grad: float32 [2048, 1024], P('row', 'col')
- input_gain_grad: float32 [1024], P('col')
- middle_gain_grad: float32 [1024], P('col')
- mixer_kernel_grad: float32 [4, 1536], P(None, 'row')
- shared_kernel_grad: float32 [4, 256], replicated
- decay_log_grad: float32 [24], P('row')
- step_bias_grad: float32 [24], P('row')
- skip_scale_grad: float32 [24], P('row')
- state_gain_grad: float32 [1536], P('row')
Inputs may be any that keep to these rules, and one draw needn't show every extreme that they name: For every micro-batch m and slot r, dealing[m, r] is a permutation of the 2 groups. For every slot r and sending group g, no group receives more than ceil(2) of g's 4 packs in slot r. lengths[m, e, r] lists in order the 4 sequences of the pack that group e holds in slot r of micro-batch m; they sum to 128.
All inputs are finite; a program needn't handle non-finite values.
Results may differ from a plain program's by a relative error of at most 0.019.
Values may be sent and summed in bfloat16 or wider, within the bound.
No kernel may reach another device: no remote copies, remote signals or barrier semaphores. Data moves between devices by JAX's collectives and lax.ppermute only.
A program may use at most 128 MiB of HBM per device.

v0:
```python
import jax
import jax.numpy as jnp
from jax import lax
from jax.sharding import PartitionSpec as P

D = 1024
QUERY_HEADS = 8
KEY_VALUE_HEADS = 2
HEAD_WIDTH = 64
NM = 24
MD = 64
STATE_WIDTH = 128
KC = 4
FF = 2048
PACK_TOKENS = 128
MB = 4
DS = 1536


epsilon = 1e-05
masked_value = -1e30
rope_base = 10000.0


def matmul_plain(left, right):
    return jnp.dot(left, right, preferred_element_type=jnp.float32)


def times_transposed(left, right):
    return lax.dot_general(
        left, right, (((1,), (1,)), ((), ())), preferred_element_type=jnp.float32
    )


def transposed_times(left, right):
    return lax.dot_general(
        left, right, (((0,), (0,)), ((), ())), preferred_element_type=jnp.float32
    )


def exact_times(left, right):
    return jnp.dot(left, right, precision=lax.Precision.HIGHEST, preferred_element_type=jnp.float32)


def exact_transposed(left, right):
    return lax.dot_general(
        left,
        right,
        (((0,), (0,)), ((), ())),
        precision=lax.Precision.HIGHEST,
        preferred_element_type=jnp.float32,
    )


def segment_info(lengths_row, count_of_rows):
    seg_ends = jnp.cumsum(lengths_row)
    places = jnp.arange(count_of_rows, dtype=jnp.int32)
    segment = jnp.sum((places[:, None] >= seg_ends[None, :]).astype(jnp.int32), axis=1)
    starts = seg_ends - lengths_row
    onehot = segment[:, None] == jnp.arange(lengths_row.shape[0], dtype=jnp.int32)[None, :]
    token_position = places - jnp.sum(jnp.where(onehot, starts[None, :], 0), axis=1)
    return (segment, token_position)


def apply_rotary(values, token_position, direction):
    half_dim = values.shape[-1] // 2
    frequency = rope_base ** (-jnp.arange(half_dim, dtype=jnp.float32) * 2.0 / values.shape[-1])
    angles = token_position.astype(jnp.float32)[:, None] * frequency[None, :]
    cosine = jnp.cos(angles)[:, None, :]
    sine_part = direction * jnp.sin(angles)[:, None, :]
    first_half = values[..., :half_dim]
    second = values[..., half_dim:]
    return jnp.concatenate(
        [first_half * cosine - second * sine_part, second * cosine + first_half * sine_part],
        axis=-1,
    )


def causal_conv(values, kernel, segment):
    summed = values * kernel[0][None, :]
    for offset in range(1, kernel.shape[0]):
        shifted = jnp.concatenate(
            [jnp.zeros((offset, values.shape[1]), values.dtype), values[:-offset]], axis=0
        )
        earlier = jnp.concatenate([jnp.full((offset,), -1, jnp.int32), segment[:-offset]], axis=0)
        summed = (
            summed
            + jnp.where((earlier == segment)[:, None], shifted, 0.0) * kernel[offset][None, :]
        )
    return summed


def shared_block(raw, kernel_cols, row_id, segment, token_position):
    rotated = apply_rotary(raw.reshape(raw.shape[0], -1, HEAD_WIDTH), token_position, 1.0).reshape(
        raw.shape
    )
    convolved = jax.nn.silu(causal_conv(raw, kernel_cols, segment))
    return jnp.where(row_id == 0, rotated, jnp.where(row_id >= 2, convolved, raw))


def silu_slope(values):
    logistic = jax.nn.sigmoid(values)
    return logistic * (1.0 + values * (1.0 - logistic))


def feature_total(values):
    return lax.psum(values, "col")


def state_total(values):
    return lax.psum(values, "row")


def rows_gather(values):
    return lax.all_gather(values, "row", axis=0, tiled=True)


def col_gather(values):
    return lax.all_gather(values, "col", axis=0, tiled=True)


def sum_to_col(whole, wide_weight, flipped):
    full_rows = lax.all_to_all(whole, "col", split_axis=0, concat_axis=1, tiled=True)
    if flipped:
        return times_transposed(full_rows, wide_weight)
    return matmul_plain(full_rows, wide_weight)


def sum_to_row(whole, wide_weight, flipped):
    full_rows = lax.all_to_all(whole, "row", split_axis=0, concat_axis=1, tiled=True)
    if flipped:
        return times_transposed(full_rows, wide_weight)
    return matmul_plain(full_rows, wide_weight)


def select_packs(carried, pieces, wanted):
    piece_count = pieces[0].shape[0]
    hit_mask = wanted[:, None] == jnp.arange(piece_count, dtype=jnp.int32)[None, :]
    results = []
    for held_pack, piece_part in zip(carried, pieces):
        swapped = jnp.swapaxes(piece_part, 0, 1)
        picked = jnp.sum(
            jnp.where(hit_mask[:, :, None, None], swapped, jnp.zeros_like(swapped)), axis=1
        )
        results.append(picked)
    return tuple(results)


def deal_in(arrivals, cot_packs, sources):
    return select_packs(
        (jnp.zeros_like(arrivals), jnp.zeros_like(cot_packs)),
        (
            lax.all_gather(arrivals[None], "dp", axis=0, tiled=True),
            lax.all_gather(cot_packs[None], "dp", axis=0, tiled=True),
        ),
        sources,
    )


def deal_out(results, grads_in, targets):
    return select_packs(
        (jnp.zeros_like(results), jnp.zeros_like(grads_in)),
        (
            lax.all_gather(results[None], "dp", axis=0, tiled=True),
            lax.all_gather(grads_in[None], "dp", axis=0, tiled=True),
        ),
        targets,
    )


def per_device(
    inputs,
    cotangent,
    mixer_in,
    mixer_out,
    expand_weight,
    shrink_weight,
    input_gain,
    middle_gain,
    mixer_kernel,
    shared_kernel,
    decay_log,
    step_bias,
    skip_scale,
    state_gain,
    dealing,
    lengths,
):
    groups = lax.axis_size("dp")
    row_devices = lax.axis_size("row")
    my_group = lax.axis_index("dp")
    own_row_index = lax.axis_index("row")
    my_col = lax.axis_index("col")
    feature_width = inputs.shape[1]
    query_w = QUERY_HEADS * HEAD_WIDTH // row_devices
    shared_w = 4 * STATE_WIDTH // row_devices
    inner_w = DS // row_devices
    hidden_w = FF // row_devices
    resident_heads = QUERY_HEADS // row_devices
    ssm_heads = NM // row_devices
    key_value_head = own_row_index * resident_heads // (QUERY_HEADS // KEY_VALUE_HEADS)
    score_scale = HEAD_WIDTH ** (-0.5)
    group_ids = jnp.arange(groups, dtype=jnp.int32)
    sources = jnp.sum(
        jnp.where(dealing[:, own_row_index, :] == my_group, group_ids[None, :], 0), axis=1
    )
    targets = dealing[:, own_row_index, my_group]
    col_weights = (
        lax.all_gather(mixer_in, "col", axis=0, tiled=True),
        lax.all_gather(expand_weight, "col", axis=0, tiled=True),
        lax.all_gather(mixer_out, "col", axis=1, tiled=True),
        lax.all_gather(shrink_weight, "col", axis=1, tiled=True),
    )
    row_weights = (
        lax.all_gather(mixer_out, "row", axis=0, tiled=True),
        lax.all_gather(shrink_weight, "row", axis=0, tiled=True),
        lax.all_gather(mixer_in, "row", axis=1, tiled=True),
        lax.all_gather(expand_weight, "row", axis=1, tiled=True),
    )
    packs_x, packs_dy = deal_in(
        inputs.reshape(MB, PACK_TOKENS, feature_width),
        cotangent.reshape(MB, PACK_TOKENS, feature_width),
        sources,
    )
    places = jnp.arange(PACK_TOKENS, dtype=jnp.int32)
    kernel_start = jnp.clip(own_row_index - 2, 0, 1) * shared_w
    kernel_cols = lax.dynamic_slice_in_dim(shared_kernel, kernel_start, shared_w, 1)
    key_selection = (jnp.arange(KEY_VALUE_HEADS, dtype=jnp.int32) == key_value_head)[None, :, None]
    decay_rates = -jnp.exp(decay_log)
    head_ids = jnp.arange(ssm_heads, dtype=jnp.int32)
    grad_mixer_in = jnp.zeros(mixer_in.shape, jnp.float32)
    grad_mixer_out = jnp.zeros(mixer_out.shape, jnp.float32)
    grad_expand = jnp.zeros(expand_weight.shape, jnp.float32)
    grad_shrink = jnp.zeros(shrink_weight.shape, jnp.float32)
    grad_input_gain = jnp.zeros(input_gain.shape, jnp.float32)
    grad_middle_gain = jnp.zeros(middle_gain.shape, jnp.float32)
    grad_mixer_kernel = jnp.zeros(mixer_kernel.shape, jnp.float32)
    grad_shared_kernel = jnp.zeros(shared_kernel.shape, jnp.float32)
    grad_decay = jnp.zeros(decay_log.shape, jnp.float32)
    grad_step_bias = jnp.zeros(step_bias.shape, jnp.float32)
    grad_skip = jnp.zeros(skip_scale.shape, jnp.float32)
    grad_state_gain = jnp.zeros(state_gain.shape, jnp.float32)
    output_packs = []
    input_packs = []
    for micro_index in range(MB):
        segment, token_position = segment_info(lengths[micro_index, my_group, my_col], PACK_TOKENS)
        allowed = (segment[:, None] == segment[None, :]) & (places[:, None] >= places[None, :])
        x_float = packs_x[micro_index].astype(jnp.float32)
        inverse1 = lax.rsqrt(feature_total(jnp.sum(x_float * x_float, axis=1)) / D + epsilon)
        normed1 = (x_float * inverse1[:, None] * input_gain[None, :]).astype(jnp.bfloat16)
        gathered1 = rows_gather(normed1)
        project = sum_to_col(gathered1, col_weights[0], False)
        gate_start = query_w + shared_w
        query_raw = project[:, :query_w]
        shared_raw = project[:, query_w:gate_start]
        gate_raw = project[:, gate_start : gate_start + inner_w]
        inner_raw = project[:, gate_start + inner_w : gate_start + 2 * inner_w]
        step_raw = project[:, gate_start + 2 * inner_w :]

        def shared_fn(raw, cols):
            return shared_block(raw, cols, own_row_index, segment, token_position)

        shared_val, shared_pull = jax.vjp(shared_fn, shared_raw, kernel_cols)
        common_projection_full = lax.all_gather(
            shared_val.astype(jnp.bfloat16), "row", axis=1, tiled=True
        )
        key_head = lax.dynamic_index_in_dim(
            common_projection_full[:, :STATE_WIDTH].reshape(
                PACK_TOKENS, KEY_VALUE_HEADS, HEAD_WIDTH
            ),
            key_value_head,
            1,
            False,
        )
        value_head = lax.dynamic_index_in_dim(
            common_projection_full[:, STATE_WIDTH : 2 * STATE_WIDTH].reshape(
                PACK_TOKENS, KEY_VALUE_HEADS, HEAD_WIDTH
            ),
            key_value_head,
            1,
            False,
        )
        in_state = common_projection_full[:, 2 * STATE_WIDTH : 3 * STATE_WIDTH]
        out_state = common_projection_full[:, 3 * STATE_WIDTH :]
        queries = apply_rotary(
            query_raw.reshape(PACK_TOKENS, resident_heads, HEAD_WIDTH), token_position, 1.0
        ).astype(jnp.bfloat16)
        scores = (
            jnp.einsum("thd,sd->hts", queries, key_head, preferred_element_type=jnp.float32)
            * score_scale
        )
        masked = jnp.where(allowed[None], scores, masked_value)
        top_score = jnp.max(masked, axis=2, keepdims=True)
        exponent = jnp.exp(masked - top_score)
        row_total = jnp.sum(exponent, axis=2, keepdims=True)
        log_total = top_score + jnp.log(row_total)
        probability = (exponent / row_total).astype(jnp.bfloat16)
        attended = jnp.einsum(
            "hts,sd->thd", probability, value_head, preferred_element_type=jnp.float32
        )

        def conv_fn(raw, kernel):
            return jax.nn.silu(causal_conv(raw, kernel, segment))

        conv_out, conv_pull = jax.vjp(conv_fn, inner_raw, mixer_kernel)
        step_input = step_raw + step_bias[None, :]
        step_size = jax.nn.softplus(step_input)
        cumulative = jnp.cumsum(step_size * decay_rates[None, :], axis=0)
        intersection = times_transposed(out_state, in_state)

        def head_parts(head_index):
            cum_head = lax.dynamic_index_in_dim(cumulative, head_index, 1, False)
            decay = jnp.exp(jnp.where(allowed, cum_head[:, None] - cum_head[None, :], masked_value))
            mixing = (decay * intersection).astype(jnp.bfloat16)
            conv_head = lax.dynamic_slice_in_dim(conv_out, head_index * MD, MD, 1)
            step_head = lax.dynamic_index_in_dim(step_size, head_index, 1, False)
            driven = (conv_head * step_head[:, None]).astype(jnp.bfloat16)
            skip_head = lax.dynamic_index_in_dim(skip_scale, head_index, 0, False)
            return (decay, mixing, conv_head, step_head, driven, skip_head)

        def ssd_forward(head_index):
            decay, mixing, conv_head, step_head, driven, skip_head = head_parts(head_index)
            return matmul_plain(mixing, driven) + skip_head * conv_head

        state_heads = lax.map(ssd_forward, head_ids)
        state_out = jnp.transpose(state_heads, (1, 0, 2)).reshape(PACK_TOKENS, inner_w)
        gate_act = jax.nn.silu(gate_raw)
        gated = state_out * gate_act
        inverse_s = lax.rsqrt(state_total(jnp.sum(gated * gated, axis=1)) / DS + epsilon)
        state_normed = gated * inverse_s[:, None] * state_gain[None, :]
        mixed = jnp.concatenate(
            [attended.reshape(PACK_TOKENS, query_w), state_normed], axis=1
        ).astype(jnp.bfloat16)
        mixed_all = col_gather(mixed)
        middle = x_float + sum_to_row(mixed_all, row_weights[0], False)
        inverse2 = lax.rsqrt(feature_total(jnp.sum(middle * middle, axis=1)) / D + epsilon)
        normed2 = (middle * inverse2[:, None] * middle_gain[None, :]).astype(jnp.bfloat16)
        gathered2 = rows_gather(normed2)
        expanded = sum_to_col(gathered2, col_weights[1], False)
        gate_part = expanded[:, :hidden_w]
        up_part = expanded[:, hidden_w:]
        hidden = (jax.nn.silu(gate_part) * up_part).astype(jnp.bfloat16)
        hidden_all = col_gather(hidden)
        output_packs.append(
            (middle + sum_to_row(hidden_all, row_weights[1], False)).astype(jnp.bfloat16)
        )
        dy_pack = packs_dy[micro_index]
        dy_all = rows_gather(dy_pack)
        grad_shrink = grad_shrink + transposed_times(hidden_all, dy_all)
        d_hidden = sum_to_col(dy_all, col_weights[3], True)
        d_gate = d_hidden * up_part * silu_slope(gate_part)
        d_up = d_hidden * jax.nn.silu(gate_part)
        d_expanded = jnp.concatenate([d_gate, d_up], axis=1).astype(jnp.bfloat16)
        d_expanded_all = col_gather(d_expanded)
        grad_expand = grad_expand + transposed_times(gathered2, d_expanded_all)
        d_normed2 = sum_to_row(d_expanded_all, row_weights[3], True)
        inner2 = feature_total(jnp.sum(d_normed2 * middle_gain[None, :] * middle, axis=1))
        d_middle = (
            dy_pack.astype(jnp.float32)
            + inverse2[:, None] * middle_gain[None, :] * d_normed2
            - middle * (inverse2 * inverse2 * inverse2 * inner2 / D)[:, None]
        )
        grad_middle_gain = grad_middle_gain + jnp.sum(
            d_normed2 * middle * inverse2[:, None], axis=0
        )
        d_branch_all = rows_gather(d_middle.astype(jnp.bfloat16))
        grad_mixer_out = grad_mixer_out + transposed_times(mixed_all, d_branch_all)
        d_mixed = sum_to_col(d_branch_all, col_weights[2], True)
        d_attended = (
            d_mixed[:, :query_w]
            .astype(jnp.bfloat16)
            .reshape(PACK_TOKENS, resident_heads, HEAD_WIDTH)
        )
        d_state_normed = d_mixed[:, query_w:]
        inner_s = state_total(jnp.sum(d_state_normed * state_gain[None, :] * gated, axis=1))
        d_gated = (
            inverse_s[:, None] * state_gain[None, :] * d_state_normed
            - gated * (inverse_s * inverse_s * inverse_s * inner_s / DS)[:, None]
        )
        grad_state_gain = grad_state_gain + jnp.sum(
            d_state_normed * gated * inverse_s[:, None], axis=0
        )
        d_state_out = d_gated * gate_act
        d_gate_raw = d_gated * state_out * silu_slope(gate_raw)

        def ssd_backward(carried, head_index):
            decay, mixing, conv_head, step_head, driven, skip_head = head_parts(head_index)
            d_out_head = lax.dynamic_slice_in_dim(d_state_out, head_index * MD, MD, 1)
            d_rounded = d_out_head.astype(jnp.bfloat16)
            d_mixing = times_transposed(d_rounded, driven)
            d_driven = transposed_times(mixing, d_rounded)
            carried = carried + (d_mixing * decay).astype(jnp.bfloat16).astype(jnp.float32)
            weighted = d_mixing * intersection * decay
            d_cum = jnp.sum(weighted, axis=1) - jnp.sum(weighted, axis=0)
            d_conv_head = d_driven * step_head[:, None] + skip_head * d_out_head
            d_step_head = jnp.sum(d_driven * conv_head, axis=1)
            d_skip_head = jnp.sum(d_out_head * conv_head)
            return (carried, (d_conv_head, d_step_head, d_cum, d_skip_head))

        d_intersection, (d_conv_heads, d_step_heads, d_cum_heads, d_skip_heads) = lax.scan(
            ssd_backward, jnp.zeros((PACK_TOKENS, PACK_TOKENS), jnp.float32), head_ids
        )
        d_conv = jnp.transpose(d_conv_heads, (1, 0, 2)).reshape(PACK_TOKENS, inner_w)
        d_rate_input = jnp.cumsum(jnp.transpose(d_cum_heads)[::-1], axis=0)[::-1]
        d_step = jnp.transpose(d_step_heads) + d_rate_input * decay_rates[None, :]
        grad_decay = grad_decay + jnp.sum(d_rate_input * step_size, axis=0) * decay_rates
        d_step_raw = d_step * jax.nn.sigmoid(step_input)
        grad_step_bias = grad_step_bias + jnp.sum(d_step_raw, axis=0)
        grad_skip = grad_skip + d_skip_heads
        d_inner_raw, d_kernel_inner = conv_pull(d_conv)
        grad_mixer_kernel = grad_mixer_kernel + d_kernel_inner
        d_out_state = exact_times(d_intersection, in_state.astype(jnp.float32))
        d_in_state = exact_transposed(d_intersection, out_state.astype(jnp.float32))
        scores_again = (
            jnp.einsum("thd,sd->hts", queries, key_head, preferred_element_type=jnp.float32)
            * score_scale
        )
        prob_float = jnp.exp(jnp.where(allowed[None], scores_again, masked_value) - log_total)
        prob_rounded = prob_float.astype(jnp.bfloat16)
        d_prob = jnp.einsum(
            "thd,sd->hts", d_attended, value_head, preferred_element_type=jnp.float32
        )
        d_value = jnp.einsum(
            "hts,thd->sd", prob_rounded, d_attended, preferred_element_type=jnp.float32
        )
        delta_row = jnp.sum(d_prob * prob_float, axis=2, keepdims=True)
        d_scores = (prob_float * (d_prob - delta_row)).astype(jnp.bfloat16)
        d_queries = (
            jnp.einsum("hts,sd->thd", d_scores, key_head, preferred_element_type=jnp.float32)
            * score_scale
        )
        d_key = (
            jnp.einsum("hts,thd->sd", d_scores, queries, preferred_element_type=jnp.float32)
            * score_scale
        )
        d_query_raw = apply_rotary(d_queries, token_position, -1.0).reshape(PACK_TOKENS, query_w)
        key_grad = jnp.where(key_selection, d_key[:, None, :], 0.0).reshape(
            PACK_TOKENS, STATE_WIDTH
        )
        value_grad = jnp.where(key_selection, d_value[:, None, :], 0.0).reshape(
            PACK_TOKENS, STATE_WIDTH
        )
        d_shared_all = jnp.concatenate([key_grad, value_grad, d_in_state, d_out_state], axis=1)
        d_shared_mine = lax.psum_scatter(
            d_shared_all.astype(jnp.bfloat16), "row", scatter_dimension=1, tiled=True
        ).astype(jnp.float32)
        d_shared_raw, d_kernel_cols = shared_pull(d_shared_mine)
        grad_shared_kernel = grad_shared_kernel + lax.dynamic_update_slice(
            jnp.zeros(shared_kernel.shape, jnp.float32), d_kernel_cols, (0, kernel_start)
        )
        d_project = jnp.concatenate(
            [d_query_raw, d_shared_raw, d_gate_raw, d_inner_raw, d_step_raw], axis=1
        ).astype(jnp.bfloat16)
        d_project_all = col_gather(d_project)
        grad_mixer_in = grad_mixer_in + transposed_times(gathered1, d_project_all)
        d_normed1 = sum_to_row(d_project_all, row_weights[2], True)
        inner1 = feature_total(jnp.sum(d_normed1 * input_gain[None, :] * x_float, axis=1))
        d_input = (
            d_middle
            + inverse1[:, None] * input_gain[None, :] * d_normed1
            - x_float * (inverse1 * inverse1 * inverse1 * inner1 / D)[:, None]
        )
        grad_input_gain = grad_input_gain + jnp.sum(d_normed1 * x_float * inverse1[:, None], axis=0)
        input_packs.append(d_input.astype(jnp.bfloat16))
    outputs, input_grad = deal_out(jnp.stack(output_packs), jnp.stack(input_packs), targets)
    summed_big = (
        lax.psum(grad_mixer_in.astype(jnp.bfloat16), "dp").astype(jnp.float32),
        lax.psum(grad_mixer_out.astype(jnp.bfloat16), "dp").astype(jnp.float32),
        lax.psum(grad_expand.astype(jnp.bfloat16), "dp").astype(jnp.float32),
        lax.psum(grad_shrink.astype(jnp.bfloat16), "dp").astype(jnp.float32),
    )
    col_start = my_col * feature_width
    row_start = own_row_index * inner_w
    head_start = own_row_index * ssm_heads
    summed_small = lax.psum(
        (
            lax.dynamic_update_slice(jnp.zeros((D,), jnp.float32), grad_input_gain, (col_start,)),
            lax.dynamic_update_slice(jnp.zeros((D,), jnp.float32), grad_middle_gain, (col_start,)),
            lax.dynamic_update_slice(
                jnp.zeros((KC, DS), jnp.float32), grad_mixer_kernel, (0, row_start)
            ),
            grad_shared_kernel,
            lax.dynamic_update_slice(jnp.zeros((NM,), jnp.float32), grad_decay, (head_start,)),
            lax.dynamic_update_slice(jnp.zeros((NM,), jnp.float32), grad_step_bias, (head_start,)),
            lax.dynamic_update_slice(jnp.zeros((NM,), jnp.float32), grad_skip, (head_start,)),
            lax.dynamic_update_slice(jnp.zeros((DS,), jnp.float32), grad_state_gain, (row_start,)),
        ),
        ("dp", "row", "col"),
    )
    return (
        outputs.reshape(MB * PACK_TOKENS, feature_width),
        input_grad.reshape(MB * PACK_TOKENS, feature_width),
        summed_big[0],
        summed_big[1],
        summed_big[2],
        summed_big[3],
        lax.dynamic_slice_in_dim(summed_small[0], col_start, feature_width, 0),
        lax.dynamic_slice_in_dim(summed_small[1], col_start, feature_width, 0),
        lax.dynamic_slice_in_dim(summed_small[2], row_start, inner_w, 1),
        summed_small[3],
        lax.dynamic_slice_in_dim(summed_small[4], head_start, ssm_heads, 0),
        lax.dynamic_slice_in_dim(summed_small[5], head_start, ssm_heads, 0),
        lax.dynamic_slice_in_dim(summed_small[6], head_start, ssm_heads, 0),
        lax.dynamic_slice_in_dim(summed_small[7], row_start, inner_w, 0),
    )


def solution(mesh):
    in_specs = (
        P(("dp", "row"), "col"),
        P(("dp", "row"), "col"),
        P("col", "row"),
        P("row", "col"),
        P("col", "row"),
        P("row", "col"),
        P("col"),
        P("col"),
        P(None, "row"),
        P(),
        P("row"),
        P("row"),
        P("row"),
        P("row"),
        P(),
        P(),
    )
    out_specs = (
        P(("dp", "row"), "col"),
        P(("dp", "row"), "col"),
        P("col", "row"),
        P("row", "col"),
        P("col", "row"),
        P("row", "col"),
        P("col"),
        P("col"),
        P(None, "row"),
        P(),
        P("row"),
        P("row"),
        P("row"),
        P("row"),
    )
    return jax.shard_map(
        per_device, mesh=mesh, in_specs=in_specs, out_specs=out_specs, check_vma=False
    )
```

profile of v0, /device:TPU:0, one launch (start us, length us, event | category | flops | bytes accessed | tf_op | source)
XLA Modules:
  0.0 1613.0 jit_solution(6709422041057176605)
XLA Ops:
  9.8 9.9 all_gather.144
  19.8 8.2 all_gather.170
  29.1 12.2 all-reduce.100
  95.0 7.8 all-to-all-done.12
  111.5 11.5 all-to-all-done.4
  172.8 33.0 %while.120 = (s32[]{:T(128)}, f32[6,128,64]{1,2,0:T(8,128)S(1)}, s32[6]{0:T(128)S(1)}, f32[128,6]{0,1:T(8,128)S(1)}, f32[128,128]{1,0:T(8,128)S(1)}, /*index=5*/...) while((s32[]{:T(128)}, f32[6,128,64]{1,2,0:T(8,128)S(1)}, ...), condition=%wide.region_11.12_spmd.clone, body=%wide.region_10.11_spmd.clone.sunk | while | flops 2244617 | bytes 170737 | solution.py:325
  210.8 24.6 %while.121 = (s32[]{:T(128)}, f32[6,128,64]{1,2,0:T(8,128)S(1)}, s32[6]{0:T(128)S(1)}, f32[128,6]{0,1:T(8,128)S(1)}, f32[128,128]{1,0:T(8,128)S(1)}, /*index=5*/...) while((s32[]{:T(128)}, f32[6,128,64]{1,2,0:T(8,128)S(1)}, ...), condition=%wide.region_25.26_spmd.clone, body=%wide.region_24.25_spmd.clone.sunk | while | flops 2244617 | bytes 169721 | solution.py:325
  236.7 33.0 %while.123 = (s32[]{:T(128)}, f32[6,128,64]{1,2,0:T(8,128)S(1)}, s32[6]{0:T(128)S(1)}, f32[128,6]{0,1:T(8,128)S(1)}, f32[128,128]{1,0:T(8,128)S(1)}, /*index=5*/...) while((s32[]{:T(128)}, f32[6,128,64]{1,2,0:T(8,128)S(1)}, ...), condition=%wide.region_53.54_spmd.clone, body=%wide.region_52.53_spmd.clone.sunk | while | flops 2244617 | bytes 170737 | solution.py:325
  270.4 32.0 %while.122 = (s32[]{:T(128)}, f32[6,128,64]{1,2,0:T(8,128)S(1)}, s32[6]{0:T(128)S(1)}, f32[128,6]{0,1:T(8,128)S(1)}, f32[128,128]{1,0:T(8,128)S(1)}, /*index=5*/...) while((s32[]{:T(128)}, f32[6,128,64]{1,2,0:T(8,128)S(1)}, ...), condition=%wide.region_39.40_spmd.clone, body=%wide.region_38.39_spmd.clone.sunk | while | flops 2244617 | bytes 169721 | solution.py:325
  302.6 7.1 all-reduce.102
  311.7 15.2 all_gather.148
  332.8 15.5 all_gather.166
  349.9 13.9 all_gather.156
  368.3 15.4 all_gather.161
  401.3 7.9 all-to-all-done.9
  409.6 9.1 all-reduce.99
  444.2 6.6 all-to-all-done.16
  470.8 10.3 all-to-all-done.10
  486.6 7.7 all-to-all-done.24
  504.2 20.6 %all-gather.46.cloned.1.call-done = bf16[512,1024]{1,0:T(8,128)(2,1)} async-done(((bf16[128,1024]{1,0:T(8,128)(2,1)}), bf16[512,1024]{1,0:T(8,128)(2,1)}) %all-gather.46.cloned.1.call-update) | async-done | bytes 1048592 | tf_op jit(solution)/shard_map/all_gather | solution.py:119
  531.4 27.1 %all-gather.36.cloned.1.call-done = bf16[256,4096]{1,0:T(8,128)(2,1)} async-done(((bf16[256,1024]{1,0:T(8,128)(2,1)}), bf16[256,4096]{1,0:T(8,128)(2,1)}) %all-gather.36.cloned.1.call-update) | async-done | bytes 2097168 | tf_op jit(solution)/shard_map/all_gather | solution.py:218
  589.1 7.7 all-to-all-done.28
  617.6 10.4 all-to-all-done.6
  632.5 8.1 all-to-all-done.20
  644.6 15.9 all_gather.152
  674.2 20.3 %all_gather.163 = bf16[512,512]{1,0:T(8,128)(2,1)S(1)} all-gather(bf16[128,512]{1,0:T(8,128)(2,1)S(1)} %copy-done.234), channel_id=1, replica_groups=mesh['dp'=2,'row'=4,'col'=4] {'col'}, dimensions={0}, use_global_device_ids=true | all-gather | bytes 655360 | tf_op jit(solution)/shard_map/all_gather | solution.py:119
  702.6 10.9 all-to-all-done.11
  725.2 7.1 all-to-all-done.29
  755.1 9.2 all-reduce.98
  766.0 6.2 all_gather.189
  782.3 6.3 all_gather.175
  795.4 19.9 %all_gather.158 = bf16[512,512]{1,0:T(8,128)(2,1)S(1)} all-gather(bf16[128,512]{1,0:T(8,128)(2,1)} %get-tuple-element.1589), channel_id=1, replica_groups=mesh['dp'=2,'row'=4,'col'=4] {'col'}, dimensions={0}, use_global_device_ids=true | all-gather | bytes 655360 | tf_op jit(solution)/shard_map/all_gather | solution.py:119
  829.8 20.6 %all_gather.168 = bf16[512,512]{1,0:T(8,128)(2,1)} all-gather(bf16[128,512]{1,0:T(8,128)(2,1)} %get-tuple-element.1591), channel_id=1, replica_groups=mesh['dp'=2,'row'=4,'col'=4] {'col'}, dimensions={0}, use_global_device_ids=true | all-gather | bytes 655360 | tf_op jit(solution)/shard_map/all_gather | solution.py:119
  854.5 6.4 all_gather.185
  894.2 7.9 all-reduce.101
  906.6 70.8 %while.124 = (s32[]{:T(128)}, f32[128,128]{1,0:T(8,128)}, f32[6,128,64]{1,2,0:T(8,128)}, f32[6,128]{1,0:T(8,128)S(1)}, f32[6,128]{1,0:T(8,128)S(1)}, /*index=5*/...) while((s32[]{:T(128)}, f32[128,128]{1,0:T(8,128)}, ...), condition=%wide.region_70.71_spmd.clone, body=%wide.region_65.70_spmd.clone.sunk | while | flops 4611849 | bytes 671550 | solution.py:400
  1007.8 79.4 %while.125 = (s32[]{:T(128)}, f32[128,128]{1,0:T(8,128)}, f32[6,128,64]{1,2,0:T(8,128)}, f32[6,128]{1,0:T(8,128)S(1)}, f32[6,128]{1,0:T(8,128)S(1)}, /*index=5*/...) while((s32[]{:T(128)}, f32[128,128]{1,0:T(8,128)}, ...), condition=%wide.region_85.86_spmd.clone, body=%wide.region_80.85_spmd.clone.sunk | while | flops 4611849 | bytes 671550 | solution.py:400
  1095.1 69.2 %while.126 = (s32[]{:T(128)}, f32[128,128]{1,0:T(8,128)}, f32[6,128,64]{1,2,0:T(8,128)}, f32[6,128]{1,0:T(8,128)S(1)}, f32[6,128]{1,0:T(8,128)S(1)}, /*index=5*/...) while((s32[]{:T(128)}, f32[128,128]{1,0:T(8,128)}, ...), condition=%wide.region_100.101_spmd.clone, body=%wide.region_95.100_spmd.clone.sunk | while | flops 4611849 | bytes 671550 | solution.py:400
  1170.1 88.2 %while.127 = (s32[]{:T(128)}, f32[128,128]{1,0:T(8,128)S(1)}, f32[6,128,64]{1,2,0:T(8,128)}, f32[6,128]{1,0:T(8,128)}, f32[6,128]{1,0:T(8,128)}, /*index=5*/f32[...) while((s32[]{:T(128)}, f32[128,128]{1,0:T(8,128)S(1)}, ...), condition=%wide.region_115.116_spmd.clone, body=%wide.region_110.115_spmd.clone.sunk | while | flops 4611849 | bytes 671550 | solution.py:400
  1314.4 19.5 %reduce-scatter.9.cloned.1.call-done = bf16[128,128]{0,1:T(8,128)(2,1)} async-done(((bf16[128,512]{0,1:T(8,128)(2,1)}), bf16[128,128]{0,1:T(8,128)(2,1)}) %reduce-scatter.9.cloned.1.call-update) | async-done | bytes 32784 | tf_op jit(solution)/shard_map/reduce_scatter | solution.py:444
  1336.1 19.8 %reduce-scatter.11.cloned.1.call-done = bf16[128,128]{0,1:T(8,128)(2,1)} async-done(((bf16[128,512]{0,1:T(8,128)(2,1)}), bf16[128,128]{0,1:T(8,128)(2,1)}) %reduce-scatter.11.cloned.1.call-update) | async-done | bytes 32784 | tf_op jit(solution)/shard_map/reduce_scatter | solution.py:444
  1395.5 8.8 all-gather
  1440.7 17.6 %all-gather.40.cloned.1.call-done = bf16[512,1030]{0,1:T(8,128)(2,1)} async-done(((bf16[128,1030]{0,1:T(8,128)(2,1)}), bf16[512,1030]{0,1:T(8,128)(2,1)}) %all-gather.40.cloned.1.call-update) | async-done | bytes 1054736 | tf_op jit(solution)/shard_map/all_gather | solution.py:119
  1461.6 26.7 %all-gather.44.cloned.1.call-done = bf16[512,1030]{0,1:T(8,128)(2,1)} async-done(((bf16[128,1030]{0,1:T(8,128)(2,1)}), bf16[512,1030]{0,1:T(8,128)(2,1)}) %all-gather.44.cloned.1.call-update) | async-done | bytes 1054736 | tf_op jit(solution)/shard_map/all_gather | solution.py:119
  1500.2 10.4 all-to-all-done.19
  1534.2 41.5 %all-reduce.96 = (f32[1024]{0:T(1024)S(1)}, f32[1024]{0:T(1024)S(1)}, f32[4,1536]{1,0:T(4,128)S(1)}, f32[4,256]{1,0:T(4,128)}, f32[24]{0:T(128)S(1)}, /*index=5*...) all-reduce(f32[1024]{0:T(1024)S(1)} %add_dynamic-update-slice_fusio, ...), channel_id=1, replica_groups=mesh['dp'=2,'row'=4,'col'=4] {'dp','row','col'}, use_global_device_ids=true, to_apply=%region_129.130 | all-reduce | flops 10824 | bytes 86592 | tf_op jit(solution)/shard_map/psum | solution.py:475
  1579.9 9.9 all-reduce.97
  1592.6 7.0 all-gather.5
  (2010 shorter events, 945.1 us)
Async XLA Ops:
  7.2 81.6 %all-gather.24.cloned.1.call-start = ((), (), s32[]{:S(2)}) async-start(), calls=%async_computation.36 | async-start | bytes 2641920 | tf_op jit(solution)/shard_map/all_gather | solution.py:209
  8.0 381.0 %all-gather.26.cloned.1.call-start = ((), (), s32[]{:S(2)}) async-start(), calls=%async_computation.37 | async-start | bytes 1310720 | tf_op jit(solution)/shard_map/all_gather | solution.py:215
  8.7 433.4 %all-gather.28.cloned.1.call-start = ((), (), s32[]{:S(2)}) async-start(), calls=%async_computation.38 | async-start | bytes 2621440 | tf_op jit(solution)/shard_map/all_gather | solution.py:210
  48.7 34.9 %all-to-all-start = ((bf16[4,128,256]{1,2,0:T(8,128)(2,1)}), bf16[4,128,256]{1,2,0:T(8,128)(2,1)S(1)}, u32[]{:S(2)}, u32[]{:S(2)}) async-start(bf16[4,128,256]{1,2,0:T(8,128)(2,1)} %copy.230), calls=%async_computation | async-start | bytes 524288 | tf_op jit(solution)/shard_map/all_to_all | solution.py:123
  52.1 398.7 %all-gather.32.cloned.1.call-start = ((), (), s32[]{:S(2)}) async-start(), calls=%async_computation.40 | async-start | bytes 1310720 | tf_op jit(solution)/shard_map/all_gather | solution.py:212
  83.6 19.3 %all-to-all-start.12 = ((bf16[4,128,256]{1,2,0:T(8,128)(2,1)}), bf16[4,128,256]{1,2,0:T(8,128)(2,1)S(1)}, u32[]{:S(2)}, u32[]{:S(2)}) async-start(bf16[4,128,256]{1,2,0:T(8,128)(2,1)} %copy.251), calls=%async_computation.12 | async-start | bytes 524288 | tf_op jit(solution)/shard_map/all_to_all | solution.py:123
  102.9 20.1 %all-to-all-start.4 = ((bf16[4,128,256]{1,2,0:T(8,128)(2,1)}), bf16[4,128,256]{1,2,0:T(8,128)(2,1)}, u32[]{:S(2)}, u32[]{:S(2)}) async-start(bf16[4,128,256]{1,2,0:T(8,128)(2,1)} %copy.237), calls=%async_computation.4 | async-start | bytes 524288 | tf_op jit(solution)/shard_map/all_to_all | solution.py:123
  123.0 18.1 %all-to-all-start.8 = ((bf16[4,128,256]{1,2,0:T(8,128)(2,1)}), bf16[4,128,256]{1,2,0:T(8,128)(2,1)}, u32[]{:S(2)}, u32[]{:S(2)}) async-start(bf16[4,128,256]{1,2,0:T(8,128)(2,1)} %copy.244), calls=%async_computation.8 | async-start | bytes 524288 | tf_op jit(solution)/shard_map/all_to_all | solution.py:123
  328.6 36.1 %all-to-all-start.1 = ((bf16[4,128,512]{1,2,0:T(8,128)(2,1)}), bf16[4,128,512]{1,2,0:T(8,128)(2,1)S(1)}, u32[]{:S(2)}, u32[]{:S(2)}) async-start(bf16[4,128,512]{1,2,0:T(8,128)(2,1)} %copy_bitcast_fusion.3), calls=%async_computation.1 | async-start | bytes 1048576 | tf_op jit(solution)/shard_map/all_to_all | solution.py:130
  364.8 19.8 %all-to-all-start.13 = ((bf16[4,128,512]{1,2,0:T(8,128)(2,1)}), bf16[4,128,512]{1,2,0:T(8,128)(2,1)S(1)}, u32[]{:S(2)}, u32[]{:S(2)}) async-start(bf16[4,128,512]{1,2,0:T(8,128)(2,1)} %copy_bitcast_fusion), calls=%async_computation.13 | async-start | bytes 1048576 | tf_op jit(solution)/shard_map/all_to_all | solution.py:130
  425.6 13.0 all-to-all-start.2
  442.0 56.4 %all-gather.34.cloned.1.call-start = ((), (), s32[]{:S(2)}) async-start(), calls=%async_computation.41 | async-start | bytes 1310720 | tf_op jit(solution)/shard_map/all_gather | solution.py:119
  460.6 20.6 %all-to-all-start.10 = ((bf16[4,128,256]{1,2,0:T(8,128)(2,1)}), bf16[4,128,256]{1,2,0:T(8,128)(2,1)S(1)}, u32[]{:S(2)}, u32[]{:S(2)}) async-start(bf16[4,128,256]{1,2,0:T(8,128)(2,1)} %copy.249), calls=%async_computation.10 | async-start | bytes 524288 | tf_op jit(solution)/shard_map/all_to_all | solution.py:123
  481.2 13.1 all-to-all-start.24
  485.2 39.5 %all-gather.46.cloned.1.call-start = ((), (), s32[]{:S(2)}) async-start(), calls=%async_computation.49 | async-start | bytes 1310720 | tf_op jit(solution)/shard_map/all_gather | solution.py:119
  497.6 60.8 %all-gather.36.cloned.1.call-start = ((), (), s32[]{:S(2)}) async-start(), calls=%async_computation.42 | async-start | bytes 2621440 | tf_op jit(solution)/shard_map/all_gather | solution.py:218
  500.7 26.4 %all-to-all-start.17 = ((bf16[4,128,1024]{1,2,0:T(8,128)(2,1)}), bf16[4,128,1024]{1,2,0:T(8,128)(2,1)S(1)}, u32[]{:S(2)}, u32[]{:S(2)}) async-start(bf16[4,128,1024]{1,2,0:T(8,128)(2,1)} %copy.259), calls=%async_computation.17 | async-start | bytes 2097152 | tf_op jit(solution)/shard_map/all_to_all | solution.py:130
  527.0 34.3 %all-to-all-start.25 = ((bf16[4,128,1024]{1,2,0:T(8,128)(2,1)}), bf16[4,128,1024]{1,2,0:T(8,128)(2,1)}, u32[]{:S(2)}, u32[]{:S(2)}) async-start(bf16[4,128,1024]{1,2,0:T(8,128)(2,1)} %copy.283), calls=%async_computation.27 | async-start | bytes 2097152 | tf_op jit(solution)/shard_map/all_to_all | solution.py:130
  571.5 13.0 all-to-all-start.14
  588.6 111.7 %all-gather.50.cloned.1.call-start = ((), (), s32[]{:S(2)}) async-start(), calls=%async_computation.52 | async-start | bytes 1310720 | tf_op jit(solution)/shard_map/all_gather | solution.py:119
  600.1 118.4 %all-gather.54.cloned.1.call-start = ((), (), s32[]{:S(2)}) async-start(), calls=%async_computation.55 | async-start | bytes 2641920 | tf_op jit(solution)/shard_map/all_gather | solution.py:217
  607.4 20.5 %all-to-all-start.6 = ((bf16[4,128,256]{1,2,0:T(8,128)(2,1)}), bf16[4,128,256]{1,2,0:T(8,128)(2,1)S(1)}, u32[]{:S(2)}, u32[]{:S(2)}) async-start(bf16[4,128,256]{1,2,0:T(8,128)(2,1)} %copy.242), calls=%async_computation.6 | async-start | bytes 524288 | tf_op jit(solution)/shard_map/all_to_all | solution.py:123
  632.0 91.0 %all-gather.42.cloned.1.call-start = ((), (), s32[]{:S(2)}) async-start(), calls=%async_computation.46 | async-start | bytes 1310720 | tf_op jit(solution)/shard_map/all_gather | solution.py:119
  643.9 92.7 %all-gather.30.cloned.1.call-start = ((), (), s32[]{:S(2)}) async-start(), calls=%async_computation.39 | async-start | bytes 1310720 | tf_op jit(solution)/shard_map/all_gather | solution.py:216
  661.6 34.0 %all-to-all-start.3 = ((bf16[4,128,512]{1,2,0:T(8,128)(2,1)}), bf16[4,128,512]{1,2,0:T(8,128)(2,1)S(1)}, u32[]{:S(2)}, u32[]{:S(2)}) async-start(bf16[4,128,512]{1,2,0:T(8,128)(2,1)} %copy.236), calls=%async_computation.3 | async-start | bytes 1048576 | tf_op jit(solution)/shard_map/all_to_all | solution.py:130
  665.1 197.6 %all-gather.38.cloned.1.call-start = ((), (), s32[]{:S(2)}) async-start(), calls=%async_computation.43 | async-start | bytes 1310720 | tf_op jit(solution)/shard_map/all_gather | solution.py:211
  695.6 17.9 %all-to-all-start.11 = ((bf16[4,128,512]{1,2,0:T(8,128)(2,1)}), bf16[4,128,512]{1,2,0:T(8,128)(2,1)S(1)}, u32[]{:S(2)}, u32[]{:S(2)}) async-start(bf16[4,128,512]{1,2,0:T(8,128)(2,1)} %copy.250), calls=%async_computation.11 | async-start | bytes 1048576 | tf_op jit(solution)/shard_map/all_to_all | solution.py:130
  713.5 18.8 %all-to-all-start.29 = ((bf16[4,128,1024]{1,2,0:T(8,128)(2,1)}), bf16[4,128,1024]{1,2,0:T(8,128)(2,1)}, u32[]{:S(2)}, u32[]{:S(2)}) async-start(bf16[4,128,1024]{1,2,0:T(8,128)(2,1)} %copy.295), calls=%async_computation.32 | async-start | bytes 2097152 | tf_op jit(solution)/shard_map/all_to_all | solution.py:130
  732.3 18.8 %all-to-all-start.21 = ((bf16[4,128,1024]{1,2,0:T(8,128)(2,1)}), bf16[4,128,1024]{1,2,0:T(8,128)(2,1)}, u32[]{:S(2)}, u32[]{:S(2)}) async-start(bf16[4,128,1024]{1,2,0:T(8,128)(2,1)} %copy.271), calls=%async_computation.22 | async-start | bytes 2097152 | tf_op jit(solution)/shard_map/all_to_all | solution.py:130
  774.1 16.4 %all-to-all-start.30 = ((bf16[4,128,256]{1,2,0:T(8,128)(2,1)}), bf16[4,128,256]{1,2,0:T(8,128)(2,1)}, u32[]{:S(2)}, u32[]{:S(2)}) async-start(bf16[4,128,256]{1,2,0:T(8,128)(2,1)} %copy.296), calls=%async_computation.33 | async-start | bytes 524288 | tf_op jit(solution)/shard_map/all_to_all | solution.py:123
  790.4 35.4 %all-to-all-start.18 = ((bf16[4,128,256]{1,2,0:T(8,128)(2,1)}), bf16[4,128,256]{1,2,0:T(8,128)(2,1)}, u32[]{:S(2)}, u32[]{:S(2)}) async-start(bf16[4,128,256]{1,2,0:T(8,128)(2,1)} %copy.260), calls=%async_computation.18 | async-start | bytes 524288 | tf_op jit(solution)/shard_map/all_to_all | solution.py:123
  825.8 39.4 %all-to-all-start.22 = ((bf16[4,128,256]{1,2,0:T(8,128)(2,1)}), bf16[4,128,256]{1,2,0:T(8,128)(2,1)}, u32[]{:S(2)}, u32[]{:S(2)}) async-start(bf16[4,128,256]{1,2,0:T(8,128)(2,1)} %copy.272), calls=%async_computation.23 | async-start | bytes 524288 | tf_op jit(solution)/shard_map/all_to_all | solution.py:123
  865.2 17.4 %all-to-all-start.26 = ((bf16[4,128,256]{1,2,0:T(8,128)(2,1)}), bf16[4,128,256]{1,2,0:T(8,128)(2,1)}, u32[]{:S(2)}, u32[]{:S(2)}) async-start(bf16[4,128,256]{1,2,0:T(8,128)(2,1)} %copy.284), calls=%async_computation.28 | async-start | bytes 524288 | tf_op jit(solution)/shard_map/all_to_all | solution.py:123
  882.6 498.2 %all-to-all-start.7 = ((bf16[4,128,512]{1,2,0:T(8,128)(2,1)}), bf16[4,128,512]{1,2,0:T(8,128)(2,1)}, u32[]{:S(2)}, u32[]{:S(2)}) async-start(bf16[4,128,512]{1,2,0:T(8,128)(2,1)} %copy.243), calls=%async_computation.7 | async-start | bytes 1048576 | tf_op jit(solution)/shard_map/all_to_all | solution.py:130
  886.8 423.1 %reduce-scatter.5.cloned.1.call-start = ((), (), s32[]{:S(2)}) async-start(), calls=%async_computation.44 | async-start | bytes 163840 | tf_op jit(solution)/shard_map/reduce_scatter | solution.py:444
  1268.6 43.5 %reduce-scatter.7.cloned.1.call-start = ((), (), s32[]{:S(2)}) async-start(), calls=%async_computation.47 | async-start | bytes 163840 | tf_op jit(solution)/shard_map/reduce_scatter | solution.py:444
  1271.8 62.1 %reduce-scatter.9.cloned.1.call-start = ((), (), s32[]{:S(2)}) async-start(), calls=%async_computation.50 | async-start | bytes 163840 | tf_op jit(solution)/shard_map/reduce_scatter | solution.py:444
  1274.9 81.0 %reduce-scatter.11.cloned.1.call-start = ((), (), s32[]{:S(2)}) async-start(), calls=%async_computation.53 | async-start | bytes 163840 | tf_op jit(solution)/shard_map/reduce_scatter | solution.py:444
  1294.0 118.9 %all-gather.52.cloned.1.call-start = ((), (), s32[]{:S(2)}) async-start(), calls=%async_computation.54 | async-start | bytes 1320960 | tf_op jit(solution)/shard_map/all_gather | solution.py:119
  1367.5 60.5 %all-gather.48.cloned.1.call-start = ((), (), s32[]{:S(2)}) async-start(), calls=%async_computation.51 | async-start | bytes 1320960 | tf_op jit(solution)/shard_map/all_gather | solution.py:119
  1380.8 13.1 all-to-all-start.15
  1384.9 73.3 %all-gather.40.cloned.1.call-start = ((), (), s32[]{:S(2)}) async-start(), calls=%async_computation.45 | async-start | bytes 1320960 | tf_op jit(solution)/shard_map/all_gather | solution.py:119
  1416.2 19.0 %all-to-all-start.31 = ((bf16[4,128,1030]{1,2,0:T(8,128)(2,1)}), bf16[4,128,1030]{1,2,0:T(8,128)(2,1)}, u32[]{:S(2)}, u32[]{:S(2)}) async-start(bf16[4,128,1030]{1,2,0:T(8,128)(2,1)} %copy.305), calls=%async_computation.35 | async-start | bytes 2113536 | tf_op jit(solution)/shard_map/all_to_all | solution.py:130
  1420.7 67.6 %all-gather.44.cloned.1.call-start = ((), (), s32[]{:S(2)}) async-start(), calls=%async_computation.48 | async-start | bytes 1320960 | tf_op jit(solution)/shard_map/all_gather | solution.py:119
  1435.2 56.4 %all-to-all-start.27 = ((bf16[4,128,1030]{1,2,0:T(8,128)(2,1)}), bf16[4,128,1030]{1,2,0:T(8,128)(2,1)}, u32[]{:S(2)}, u32[]{:S(2)}) async-start(bf16[4,128,1030]{1,2,0:T(8,128)(2,1)} %copy.293), calls=%async_computation.30 | async-start | bytes 2113536 | tf_op jit(solution)/shard_map/all_to_all | solution.py:130
  1491.6 19.0 %all-to-all-start.19 = ((bf16[4,128,1030]{1,2,0:T(8,128)(2,1)}), bf16[4,128,1030]{1,2,0:T(8,128)(2,1)}, u32[]{:S(2)}, u32[]{:S(2)}) async-start(bf16[4,128,1030]{1,2,0:T(8,128)(2,1)} %copy.269), calls=%async_computation.20 | async-start | bytes 2113536 | tf_op jit(solution)/shard_map/all_to_all | solution.py:130
  1510.6 18.0 %all-to-all-start.23 = ((bf16[4,128,1030]{1,2,0:T(8,128)(2,1)}), bf16[4,128,1030]{1,2,0:T(8,128)(2,1)S(1)}, u32[]{:S(2)}, u32[]{:S(2)}) async-start(bf16[4,128,1030]{1,2,0:T(8,128)(2,1)} %copy.281), calls=%async_computation.25 | async-start | bytes 2113536 | tf_op jit(solution)/shard_map/all_to_all | solution.py:130
  1514.2 86.6 %all-reduce.106.cloned.1.call-start = ((), (), s32[]{:S(2)}) async-start(), calls=%async_computation.56 | async-start | bytes 3153920 | tf_op jit(solution)/shard_map/psum | solution.py:467
  (533 other events, 8114.8 us)
Sparse Core Ops, SparseCore 0:
  9.6 55.0 all-gather.23
  66.3 14.9 all-gather.25
  82.9 60.1 all-gather.27
  144.5 29.2 all-gather.31
  454.1 33.1 all-gather.33
  497.7 26.9 all-gather.45
  526.3 32.0 all-gather.35
  600.2 32.0 all-gather.49
  633.8 21.5 all-gather.53
  657.4 35.3 all-gather.41
  694.4 20.6 all-gather.29
  716.4 29.2 all-gather.37
  1268.7 21.2 reduce-scatter.4
  1292.4 19.5 reduce-scatter.6
  1314.3 19.5 reduce-scatter.8
  1336.3 19.5 reduce-scatter.10
  1367.6 30.3 all-gather.51
  1399.4 28.6 all-gather.47
  1429.6 28.6 all-gather.39
  1459.7 28.6 all-gather.43
  1518.1 52.4 all-reduce.105
where the time goes:
time: 1640 us; the launch traced here: 1610 us
  blocking collectives  385 us (23%)
  local copies, waits for them, and re-layouts  299 us (18%)
  waiting for transfers between devices  272 us (17%)
  matrix products  246 us (15%)
  other arithmetic  140 us (9%)
  starting transfers between devices  126 us (8%)
  loops' own time  122 us (7%)
  between operations  21.7 us (1%)
    all_gather x8, blocking collectives, col_gather(): return lax.all_gather(values, 'col', axis=0, tiled=True)  137 us
    all_gather x16, blocking collectives, rows_gather(): return lax.all_gather(values, 'row', axis=0, tiled=True)  95.6 us
    dot_general x40, matrix products, transposed_times(): lax.dot_general(left, right, (((0,), (0,)), ((), ())), preferred_element_...  80.2 us
    dot_general x44, matrix products, times_transposed(): lax.dot_general(left, right, (((1,), (1,)), ((), ())), preferred_element_...  76.3 us
    all_to_all x16, waiting for transfers between devices, sum_to_col(): lax.all_to_all(whole, 'col', split_axis=0, concat_axis=1, tiled=True)  75.3 us
    all_gather x8, waiting for transfers between devices, col_gather(): return lax.all_gather(values, 'col', axis=0, tiled=True)  68.4 us
    all_to_all x16, starting transfers between devices, sum_to_col(): lax.all_to_all(whole, 'col', split_axis=0, concat_axis=1, tiled=True)  62.8 us
    all_to_all x16, starting transfers between devices, sum_to_row(): lax.all_to_all(whole, 'row', split_axis=0, concat_axis=1, tiled=True)  62.2 us
  transfers between devices with their start and end apart: 53, of which 26 were waited for; matrix products, arithmetic and copies ran while one was open for 40% of the time, Pallas kernels for 0%

commit v1 on v0

v1 whole, which is shorter than its diff:
```python
import jax
import jax.numpy as jnp
from jax import lax
from jax.experimental import pallas as pl
from jax.experimental.pallas import tpu as pltpu
from jax.sharding import PartitionSpec as P

D = 1024
QUERY_HEADS = 8
KEY_VALUE_HEADS = 2
HEAD_WIDTH = 64
NM = 24
MD = 64
STATE_WIDTH = 128
KC = 4
FF = 2048
T = 128
MB = 4
DS = 1536
SLOTS = 4
TT = SLOTS * T
QW = 128
IW = 384
HW = 512
PAIRS = 3
EPS = 1e-05
NEG = -1e30
ROPE_BASE = 10000.0
F32 = jnp.float32
BF = jnp.bfloat16
HI = lax.Precision.HIGHEST


def nn(a, b):
    return lax.dot_general(a, b, (((1,), (0,)), ((), ())), preferred_element_type=F32)


def nt(a, b):
    return lax.dot_general(a, b, (((1,), (1,)), ((), ())), preferred_element_type=F32)


def tn(a, b):
    return lax.dot_general(a, b, (((0,), (0,)), ((), ())), preferred_element_type=F32)


def nn_exact(a, b):
    return lax.dot_general(
        a, b, (((1,), (0,)), ((), ())), precision=HI, preferred_element_type=F32
    )


def lanes(rows=T):
    return lax.broadcasted_iota(jnp.int32, (rows, 128), 1)


def rows_of(j, n=T):
    return slice(j * n, (j + 1) * n)


def sigmoid(v):
    return 1.0 / (1.0 + jnp.exp(-v))


def silu_slope(v, s):
    return s * (1.0 + v * (1.0 - s))


def swap_halves(v):
    lane = lanes(v.shape[0])
    return jnp.where((lane % 64) < 32, pltpu.roll(v, 96, 1), pltpu.roll(v, 32, 1))


def conv(v, k, pos):
    acc = v * k[0:1]
    for j in range(1, KC):
        acc = acc + jnp.where(pos >= j, pltpu.roll(v, j, 0), 0.0) * k[j : j + 1]
    return acc


def tile_lanes(v, n):
    return jnp.concatenate([v] * n, axis=1)


def conv_back(dcv, v, k, pos):
    n = v.shape[0]
    dv = dcv * k[0:1]
    dk = [jnp.sum(dcv * v, axis=0, keepdims=True)]
    for j in range(1, KC):
        m = jnp.where(pos >= j, dcv, 0.0)
        dv = dv + pltpu.roll(m, n - j, 0) * k[j : j + 1]
        dk.append(jnp.sum(m * pltpu.roll(v, j, 0), axis=0, keepdims=True))
    return dv, dk


def hi_lo(total):
    wide = jnp.broadcast_to(total, (total.shape[0], 128))
    high = wide.astype(BF).astype(F32)
    return jnp.where(lanes(total.shape[0]) < 64, high, wide - high).astype(BF)


def from_hi_lo(v):
    v = v.astype(F32)
    return v + pltpu.roll(v, 64, 1)


def pick(scal, pieces, block, j):
    k_of = scal[0] ^ block
    out = pieces[0][rows_of(j)].astype(F32)
    for k in range(1, SLOTS):
        out = jnp.where(k_of == k, pieces[k][rows_of(j ^ k)].astype(F32), out)
    return out


def both_heads(v, kv):
    keep = (lanes(v.shape[0]) // 64) == kv
    return jnp.where(keep, v, pltpu.roll(v, 64, 1))


def split_pair(v):
    low = lanes(v.shape[0]) < 64
    zero = jnp.zeros_like(v)
    return jnp.concatenate([jnp.where(low, v, zero), jnp.where(low, zero, v)], axis=0)


def join_pair(v):
    n = v.shape[0] // 2
    return jnp.where(lanes(n) < 64, v[:n], v[n:])


def fold_pair(v, kv):
    total = v + pltpu.roll(v, 64, 1)
    return jnp.where((lanes(v.shape[0]) // 64) == kv, total, 0.0)


def mask_of(pos):
    ti = lax.broadcasted_iota(jnp.int32, (T, T), 0)
    si = lax.broadcasted_iota(jnp.int32, (T, T), 1)
    d = (ti - si).astype(F32)
    return (d >= 0) & (d <= pos)


def head_col(v, h):
    return jnp.broadcast_to(v[:, h : h + 1], (v.shape[0], 128))


def pair_cols(v, k):
    return jnp.where(lanes(v.shape[0]) < 64, head_col(v, 2 * k), head_col(v, 2 * k + 1))


def tri(upper):
    a = lax.broadcasted_iota(jnp.int32, (T, T), 0)
    b = lax.broadcasted_iota(jnp.int32, (T, T), 1)
    return jnp.where((b >= a) if upper else (b <= a), 1.0, 0.0).astype(F32)


def prep_body(scal, own, peer, gain, x_ref, n_ref, inv_ref):
    mine = scal[1] == 1
    total = jnp.zeros((T, 1), F32)
    for c in range(4):
        v = jnp.where(mine, own[c].astype(F32), peer[c].astype(F32))
        x_ref[:, c * 256 : (c + 1) * 256] = v.astype(BF)
        total = total + jnp.sum(v * v, axis=1, keepdims=True)
    inv = lax.rsqrt(total / D + EPS)
    inv_ref[...] = jnp.broadcast_to(inv, (T, 128))
    n_ref[...] = (x_ref[...].astype(F32) * inv * gain[...]).astype(BF)


def proj1_body(scal, x0, x1, x2, x3, w, pos, cs, sn, kc, x_ref, q_ref, raw_ref, sh_ref):
    for j, piece in enumerate((x0, x1, x2, x3)):
        x_ref[rows_of(j)] = piece[...]
    qs = nn(x_ref[...], w[:, 0:256])
    r = scal[0]
    for j in range(SLOTS):
        rr = rows_of(j)
        q = qs[rr, 0:128]
        v = qs[rr, 128:256]
        q_ref[rr] = (q * cs[rr] + swap_halves(q) * sn[rr]).astype(BF)
        raw_ref[rr] = v
        rotated = v * cs[rr] + swap_halves(v) * sn[rr]
        cv = conv(v, kc[...], pos[rr])
        act = cv * sigmoid(cv)
        sh_ref[rr] = jnp.where(r == 0, rotated, jnp.where(r >= 2, act, v)).astype(BF)


def proj2_body(x, w, pos, mk, bias, z_ref, u_ref, w_ref, cv_ref):
    for n in range(3):
        res = nn(x[...], w[:, 256 * (n + 1) : 256 * (n + 2)])
        for half in range(2):
            part = res[:, half * 128 : (half + 1) * 128]
            i = 2 * n + half
            if i < 3:
                z_ref[:, i * 128 : (i + 1) * 128] = part
            else:
                i = i - 3
                cc = slice(i * 128, (i + 1) * 128)
                u_ref[:, cc] = part
                for j in range(SLOTS):
                    rr = rows_of(j)
                    cv_ref[rr, cc] = conv(part[rr], mk[:, cc], pos[rr])
    w_ref[...] = jnp.zeros_like(w_ref)
    w_ref[:, 0:6] = nn(x[...], w[:, 1024:1030])
    w_ref[...] = w_ref[...] + bias[...]


def softplus(v):
    return jnp.maximum(v, 0.0) + jnp.log1p(jnp.exp(-jnp.abs(v)))


def mixf_body(
    scal, q, p0, p1, p2, p3, pos, z, cv, wi, rate, skip, gain, wo,
    att_ref, prob_ref, state_ref, send_ref, keep_ref, gg_ref, st_ref,
):
    pieces = (p0, p1, p2, p3)
    kv = scal[0] // 2
    low = tri(False)
    for j in range(SLOTS):
        rr = rows_of(j)
        allowed = mask_of(pos[rr])
        allowed2 = jnp.concatenate([allowed, allowed], axis=0)
        keys = both_heads(pick(scal, pieces, 0, j), kv).astype(BF)
        vals = both_heads(pick(scal, pieces, 1, j), kv).astype(BF)
        q2 = split_pair(q[rr].astype(F32)).astype(BF)
        score = jnp.where(allowed2, nt(q2, keys) * (HEAD_WIDTH**-0.5), NEG)
        e = jnp.exp(score - jnp.max(score, axis=1, keepdims=True))
        prob = e / jnp.sum(e, axis=1, keepdims=True)
        prob_ref[rows_of(j, 2 * T)] = prob
        att_ref[rr] = join_pair(nn(prob.astype(BF), vals)).astype(BF)
        b_in = pick(scal, pieces, 2, j).astype(BF)
        c_out = pick(scal, pieces, 3, j).astype(BF)
        inter = nt(c_out, b_in)
        step = softplus(wi[rr])
        cum = nn_exact(low, step * rate[...])
        cum_t = jnp.transpose(cum)
        total = jnp.zeros((T, 128), F32)
        for k in range(PAIRS):
            cc = slice(k * 128, (k + 1) * 128)
            mix = []
            for h in (2 * k, 2 * k + 1):
                gap = head_col(cum, h) - cum_t[h : h + 1, :]
                mix.append((jnp.exp(jnp.where(allowed, gap, NEG)) * inter).astype(BF))
            c = cv[rr, cc]
            inner = c * sigmoid(c)
            driven = (inner * pair_cols(step, k)).astype(BF)
            state = join_pair(nn(jnp.concatenate(mix, axis=0), driven)) + skip[:, cc] * inner
            state_ref[rr, cc] = state
            zz = z[rr, cc]
            gated = state * (zz * sigmoid(zz))
            total = total + gated * gated
            gg_ref[rr, cc] = (gated * gain[:, cc]).astype(BF)
        st_ref[rr] = jnp.sum(total, axis=1, keepdims=True) + jnp.zeros((T, 128), F32)
    for c in range(4):
        pa = nn(att_ref[...], wo[c, 0:128, :])
        ps = nn(gg_ref[...], wo[c, 128:512, :])
        for off, part in ((0, pa), (1024, ps)):
            cc = slice(off + c * 256, off + (c + 1) * 256)
            for i in range(2):
                keep_ref[i, :, cc] = part[rows_of(2 * i)]
                send_ref[i, :, cc] = part[rows_of(2 * i + 1)].astype(BF)
    for i in range(2):
        keep_ref[i, :, 2048:2176] = hi_lo(st_ref[rows_of(2 * i), 0:1]).astype(F32)
        send_ref[i, :, 2048:2176] = hi_lo(st_ref[rows_of(2 * i + 1), 0:1])


def rsa_body(keep, recv, s0_ref, s2_ref):
    s0_ref[...] = keep[0] + recv[0].astype(F32)
    total = keep[1] + recv[1].astype(F32)
    width = s2_ref.shape[1]
    s2_ref[...] = total.astype(BF)
    if width == 2176:
        st = from_hi_lo(total[:, 2048:2176])
        s2_ref[:, 2048:2176] = hi_lo(st[:, 0:1])


def mid_body(s0, recv, x, gain, mid_ref, n_ref, zs_ref, inv_ref):
    zs = s0[:, 1024:2048] + recv[:, 1024:2048].astype(F32)
    st = from_hi_lo(s0[:, 2048:2176]) + from_hi_lo(recv[:, 2048:2176])
    scale = lax.rsqrt(st[:, 0:1] / DS + EPS)
    zs_ref[...] = zs
    mid = x[...].astype(F32) + s0[:, 0:1024] + recv[:, 0:1024].astype(F32) + scale * zs
    mid_ref[...] = mid
    inv = lax.rsqrt(jnp.sum(mid * mid, axis=1, keepdims=True) / D + EPS)
    inv_ref[...] = jnp.broadcast_to(inv, (T, 128))
    n_ref[:, 0:1024] = (mid * inv * gain[...]).astype(BF)
    n_ref[:, 1024:1152] = hi_lo(scale)


def ffn_body(
    n0, n1, n2, n3, y0, y1, y2, y3, we, ws,
    x_ref, y_ref, is_ref, h_ref, de_ref, send_ref, keep_ref,
):
    for j, (n, y) in enumerate(((n0, y0), (n1, y1), (n2, y2), (n3, y3))):
        rr = rows_of(j)
        x_ref[rr] = n[:, 0:1024]
        is_ref[rr] = from_hi_lo(n[:, 1024:1152])
        y_ref[rr] = y[...]
    for n in range(2):
        cc = slice(n * 256, (n + 1) * 256)
        uc = slice(HW + n * 256, HW + (n + 1) * 256)
        g = nn(x_ref[...], we[:, cc])
        u = nn(x_ref[...], we[:, uc])
        dh = jnp.zeros((TT, 256), F32)
        for c in range(4):
            dh = dh + nt(y_ref[:, c * 256 : (c + 1) * 256], ws[c, cc, :])
        s = sigmoid(g)
        act = g * s
        h_ref[:, cc] = (act * u).astype(BF)
        de_ref[:, cc] = (dh * u * silu_slope(g, s)).astype(BF)
        de_ref[:, uc] = (dh * act).astype(BF)
    for c in range(4):
        cc = slice(c * 256, (c + 1) * 256)
        part = nt(de_ref[...], we[cc, :])
        for i in range(2):
            keep_ref[i, :, cc] = part[rows_of(2 * i)]
            send_ref[i, :, cc] = part[rows_of(2 * i + 1)].astype(BF)


def outp_body(h, ws, send_ref, keep_ref):
    for c in range(4):
        cc = slice(c * 256, (c + 1) * 256)
        part = nn(h[...], ws[c])
        for i in range(2):
            keep_ref[i, :, cc] = part[rows_of(2 * i)]
            send_ref[i, :, cc] = part[rows_of(2 * i + 1)].astype(BF)


def fin_body(s0, recv, mid, o_ref):
    o_ref[...] = (mid[...] + s0[...] + recv[...].astype(F32)).astype(BF)


def dmid_body(s0, recv, mid, inv, dy, gain, zs, dm_ref, db_ref, gg_ref):
    dn = s0[...] + recv[...].astype(F32)
    m = mid[...]
    i2 = inv[:, 0:1]
    g = gain[...]
    inner = jnp.sum(dn * g * m, axis=1, keepdims=True)
    dm = dy[...].astype(F32) + i2 * g * dn - m * (i2 * i2 * i2 * inner / D)
    dm_ref[...] = dm
    gg_ref[...] = jnp.sum(dn * m * i2, axis=0, keepdims=True)
    db = dm.astype(BF)
    db_ref[:, 0:1024] = db
    db_ref[:, 1024:1152] = hi_lo(jnp.sum(db.astype(F32) * zs[...], axis=1, keepdims=True))


def mixb_body(
    scal, b0, b1, b2, b3, q, p0, p1, p2, p3, pos, cs, sn, prob, z, u, cv, state, wi, isb,
    att, rate, skip, gain, mk, wo,
    d_ref, mixed_ref, dq_ref, dz_ref, du_ref, dw_ref, send_ref, keep_ref,
    dmk_ref, dgain_ref, dskip_ref, dlog_ref, dbias_ref,
    dmix, blocks,
):
    pieces = (p0, p1, p2, p3)
    r = scal[0]
    kv = r // 2
    low, up = tri(False), tri(True)
    seg_row = lax.broadcasted_iota(jnp.int32, (IW, 128), 0) // 64
    seg_col = lax.broadcasted_iota(jnp.int32, (IW, 128), 1)
    heads = jnp.where(seg_row == seg_col, 1.0, 0.0).astype(F32)
    dmk_ref[...] = jnp.zeros_like(dmk_ref)
    dgain_ref[...] = jnp.zeros_like(dgain_ref)
    dskip_ref[...] = jnp.zeros_like(dskip_ref)
    dlog_ref[...] = jnp.zeros_like(dlog_ref)
    dbias_ref[...] = jnp.zeros_like(dbias_ref)
    for j, b in enumerate((b0, b1, b2, b3)):
        d_ref[rows_of(j)] = b[:, 0:1024]
    for n in range(2):
        cc = slice(n * 256, (n + 1) * 256)
        acc = jnp.zeros((TT, 256), F32)
        for c in range(4):
            acc = acc + nt(d_ref[:, c * 256 : (c + 1) * 256], wo[c, cc, :])
        dmix[:, cc] = acc
    for j, b in enumerate((b0, b1, b2, b3)):
        rr = rows_of(j)
        r2 = rows_of(j, 2 * T)
        allowed = mask_of(pos[rr])
        keys = both_heads(pick(scal, pieces, 0, j), kv).astype(BF)
        vals = both_heads(pick(scal, pieces, 1, j), kv).astype(BF)
        q2 = split_pair(q[rr].astype(F32)).astype(BF)
        da2 = split_pair(dmix[rr, 0:128]).astype(BF)
        pf = prob[r2]
        dprob = nt(da2, vals)
        delta = jnp.sum(dprob * pf, axis=1, keepdims=True)
        dscore = (pf * (dprob - delta)).astype(BF)
        scale = HEAD_WIDTH**-0.5
        dqr = join_pair(nn(dscore, keys)) * scale
        dq_ref[rr] = (dqr * cs[rr] - swap_halves(dqr) * sn[rr]).astype(BF)
        blocks[0] = fold_pair(tn(dscore, q2) * scale, kv)
        blocks[1] = fold_pair(tn(pf.astype(BF), da2), kv)
        b_in = pick(scal, pieces, 2, j).astype(BF)
        c_out = pick(scal, pieces, 3, j).astype(BF)
        inter = nt(c_out, b_in)
        sin = wi[rr]
        step = softplus(sin)
        cum = nn_exact(low, step * rate[...])
        cum_t = jnp.transpose(cum)
        scale_s = isb[rr, 0:1]
        inner_s = from_hi_lo(b[:, 1024:1152])[:, 0:1]
        coef = scale_s * scale_s * scale_s * inner_s / DS
        dinter = jnp.zeros((T, T), F32)
        dstep = jnp.zeros((T, 128), F32)
        dcum = jnp.zeros((T, 128), F32)
        mixed_ref[rr, 0:128] = att[rr]
        for k in range(PAIRS):
            cc = slice(k * 128, (k + 1) * 128)
            mc = slice((k + 1) * 128, (k + 2) * 128)
            c = cv[rr, cc]
            sc = sigmoid(c)
            inner = c * sc
            step_k = pair_cols(step, k)
            driven = (inner * step_k).astype(BF)
            st = state[rr, cc]
            zz = z[rr, cc]
            sz = sigmoid(zz)
            act = zz * sz
            gated = st * act
            dns = dmix[rr, mc]
            gk = gain[:, cc]
            mixed_ref[rr, mc] = (gated * scale_s * gk).astype(BF)
            dgated = scale_s * gk * dns - gated * coef
            dgain_ref[:, cc] += jnp.sum(dns * gated * scale_s, axis=0, keepdims=True)
            dz_ref[rr, cc] = (dgated * st * silu_slope(zz, sz)).astype(BF)
            dst = dgated * act
            dr2 = split_pair(dst).astype(BF)
            dmixing = nt(dr2, driven)
            mix = []
            for i, h in enumerate((2 * k, 2 * k + 1)):
                gap = head_col(cum, h) - cum_t[h : h + 1, :]
                decay = jnp.exp(jnp.where(allowed, gap, NEG))
                mix.append((decay * inter).astype(BF))
                dinter = dinter + (dmixing[rows_of(i)] * decay).astype(BF).astype(F32)
            ddriven = tn(jnp.concatenate(mix, axis=0), dr2)
            sk = skip[:, cc]
            dinner = ddriven * step_k + sk * dst
            dskip_ref[:, cc] += jnp.sum(dst * inner, axis=0, keepdims=True)
            dr = dst.astype(BF).astype(F32)
            cross = dr * (st - sk * inner) - driven.astype(F32) * ddriven
            dcum = dcum + nn_exact(cross, heads[cc])
            dstep = dstep + nn_exact(ddriven * inner, heads[cc])
            dcv = dinner * silu_slope(c, sc)
            dv, dk = conv_back(dcv, u[rr, cc], mk[:, cc], pos[rr])
            du_ref[rr, cc] = dv.astype(BF)
            for t in range(KC):
                dmk_ref[t : t + 1, cc] += dk[t]
        dib = dinter.astype(BF)
        blocks[2] = tn(dib, c_out)
        blocks[3] = nn(dib, b_in)
        drate = nn_exact(up, dcum)
        dstep = dstep + drate * rate[...]
        dlog_ref[...] += jnp.sum(drate * step, axis=0, keepdims=True) * rate[...]
        dw = dstep * sigmoid(sin)
        dw_ref[rr] = dw.astype(BF)
        dbias_ref[...] += jnp.sum(dw, axis=0, keepdims=True)
        for i in range(2):
            keep_ref[i, rr] = blocks[r ^ (2 * i)]
            send_ref[i, rr] = blocks[r ^ (2 * i + 1)].astype(BF)


def rss_body(keep, recv, s0_ref, s2_ref):
    for j in range(SLOTS):
        rr, other = rows_of(j), rows_of(j ^ 1)
        s0_ref[rr] = keep[0, rr] + recv[0, other].astype(F32)
        s2_ref[rr] = (keep[1, rr] + recv[1, other].astype(F32)).astype(BF)


def dproj_body(
    scal, s0, recv, raw, pos, cs, sn, kc, dq, dz, du, dw, w,
    dp_ref, send_ref, keep_ref, dkc_ref,
):
    r = scal[0]
    dkc_ref[...] = jnp.zeros_like(dkc_ref)
    for j in range(SLOTS):
        rr = rows_of(j)
        d = s0[rr] + recv[rows_of(j ^ 2)].astype(F32)
        rotated = d * cs[rr] - swap_halves(d) * sn[rr]
        v = raw[rr]
        cv = conv(v, kc[...], pos[rr])
        dcv = d * silu_slope(cv, sigmoid(cv))
        dv, dk = conv_back(dcv, v, kc[...], pos[rr])
        out = jnp.where(r == 0, rotated, jnp.where(r >= 2, dv, d))
        dp_ref[rr, 128:256] = out.astype(BF)
        for t in range(KC):
            dkc_ref[t : t + 1, :] += jnp.where(r >= 2, dk[t], 0.0)
    dp_ref[:, 0:128] = dq[...]
    dp_ref[:, 256:640] = dz[...]
    dp_ref[:, 640:1024] = du[...]
    dp_ref[:, 1024:1030] = dw[:, 0:6]
    for c in range(4):
        cc = slice(c * 256, (c + 1) * 256)
        part = nt(dp_ref[:, 0:1024], w[cc, 0:1024]) + nt(dp_ref[:, 1024:1030], w[cc, 1024:1030])
        for i in range(2):
            keep_ref[i, :, cc] = part[rows_of(2 * i)]
            send_ref[i, :, cc] = part[rows_of(2 * i + 1)].astype(BF)


def dx_body(s0, recv, dm, x, inv, gain, o_ref, gg_ref):
    dn = s0[...] + recv[...].astype(F32)
    xf = x[...].astype(F32)
    i1 = inv[:, 0:1]
    g = gain[...]
    inner = jnp.sum(dn * g * xf, axis=1, keepdims=True)
    o_ref[...] = (dm[...] + i1 * g * dn - xf * (i1 * i1 * i1 * inner / D)).astype(BF)
    gg_ref[...] = jnp.sum(dn * xf * i1, axis=0, keepdims=True)


def kernel(body, outs, args, scal=None, scratch=(), flops=0, mib=40):
    shapes = [jax.ShapeDtypeStruct(s, d) for s, d in outs]
    moved = sum(a.size * a.dtype.itemsize for a in (*args, *shapes))
    vm = pl.BlockSpec(memory_space=pltpu.VMEM)
    specs = [vm] * len(args)
    if scal is not None:
        specs = [pl.BlockSpec(memory_space=pltpu.SMEM), *specs]
        args = (scal, *args)
    return pl.pallas_call(
        body,
        out_shape=shapes,
        in_specs=specs,
        out_specs=[vm] * len(outs),
        scratch_shapes=list(scratch),
        compiler_params=pltpu.CompilerParams(vmem_limit_bytes=mib << 20),
        cost_estimate=pl.CostEstimate(flops=flops, bytes_accessed=moved, transcendentals=0),
    )(*args)


def xor_row(v, k):
    return lax.ppermute(v, "row", [(i, i ^ k) for i in range(SLOTS)])


def gather_row(v):
    a = xor_row(v, 1)
    b = xor_row(v, 2)
    return v, a, b, xor_row(b, 1)


def scatter_row(send, keep):
    recv = xor_row(send, 1)
    width = keep.shape[2]
    s0, s2 = kernel(rsa_body, [((T, width), F32), ((T, width), BF)], (keep, recv), mib=16)
    return s0, xor_row(s2, 2)


def per_device(
    inputs,
    cotangent,
    mixer_in,
    mixer_out,
    expand_weight,
    shrink_weight,
    input_gain,
    middle_gain,
    mixer_kernel,
    shared_kernel,
    decay_log,
    step_bias,
    skip_scale,
    state_gain,
    dealing,
    lengths,
):
    groups = lax.axis_size("dp")
    g = lax.axis_index("dp")
    r = lax.axis_index("row")
    c = lax.axis_index("col")

    def gather_col(v):
        return lax.all_gather(v, "col", axis=0, tiled=True)

    w_in = gather_col(mixer_in)
    w_out = gather_col(mixer_out).reshape(4, 512, 256)
    w_ex = gather_col(expand_weight)
    w_sh = gather_col(shrink_weight).reshape(4, 512, 256)
    gains = lax.all_gather(jnp.stack([input_gain, middle_gain]), "col", axis=1, tiled=True)
    gain1, gain2 = gains[0:1], gains[1:2]

    ids = jnp.arange(groups, dtype=jnp.int32)
    deal_mine = lax.dynamic_index_in_dim(
        lax.dynamic_index_in_dim(dealing, c, 0, False), r, 0, False
    )
    source = jnp.sum(jnp.where(deal_mine == g, ids, 0))
    target = jnp.sum(jnp.where(ids == g, deal_mine, 0))

    def over_dp(v, wanted):
        if groups == 2:
            return v, lax.ppermute(v, "dp", [(0, 1), (1, 0)])
        whole = lax.all_gather(v, "dp", axis=0, tiled=False)
        sel = lax.dynamic_index_in_dim(whole, wanted, 0, False)
        return sel, sel

    scal = jnp.stack(
        [r, (source == g).astype(jnp.int32), (target == g).astype(jnp.int32), c]
    ).astype(jnp.int32)

    def deal_in(v):
        mine = lax.all_to_all(v.reshape(MB, T, 256), "col", split_axis=0, concat_axis=0, tiled=True)
        return over_dp(mine, source)

    def deal_out(v):
        own, peer = over_dp(v, target)
        sel = jnp.where(scal[2] == 1, own, peer) if groups == 2 else own
        parts = jnp.transpose(sel.reshape(T, 4, 256), (1, 0, 2))
        back = lax.all_to_all(parts, "col", split_axis=0, concat_axis=0, tiled=True)
        return back.reshape(MB * T, 256)

    own_x, peer_x = deal_in(inputs)
    x, n1, inv1 = kernel(
        prep_body,
        [((T, D), BF), ((T, D), BF), ((T, 128), F32)],
        (own_x, peer_x, gain1),
        scal,
        mib=16,
    )
    own_y, peer_y = deal_in(cotangent)
    dy = jnp.transpose(jnp.where(scal[1] == 1, own_y, peer_y), (1, 0, 2)).reshape(T, D)

    slot_ids = r ^ jnp.arange(SLOTS, dtype=jnp.int32)
    group_lengths = lax.dynamic_index_in_dim(
        lax.dynamic_index_in_dim(lengths, c, 0, False), g, 0, False
    )
    here = slot_ids[:, None] == jnp.arange(SLOTS, dtype=jnp.int32)[None, :]
    lens = jnp.sum(jnp.where(here[:, :, None], group_lengths[None], 0), axis=1)
    count = lens.shape[1]
    before = jnp.arange(count)[:, None] >= jnp.arange(count)[None, :]
    ends = jnp.sum(jnp.where(before[None], lens[:, None, :], 0), axis=2)
    places = jnp.arange(T, dtype=jnp.int32)
    past = places[None, :, None] >= ends[:, None, :]
    position = places[None, :] - jnp.sum(jnp.where(past, lens[:, None, :], 0), axis=2)
    posf = position.reshape(TT).astype(F32)
    pos = jnp.broadcast_to(posf[:, None], (TT, 128))
    freq = ROPE_BASE ** (-jnp.arange(32, dtype=F32) * 2.0 / HEAD_WIDTH)
    angle = posf[:, None] * freq[None, :]
    cosine, sine = jnp.cos(angle), jnp.sin(angle)
    cs = jnp.concatenate([cosine] * 4, axis=1)
    sn = jnp.concatenate([-sine, sine, -sine, sine], axis=1)
    kernel_start = jnp.clip(r - 2, 0, 1) * 128
    kc = lax.dynamic_slice_in_dim(shared_kernel, kernel_start, 128, 1)

    def pad_lanes(v):
        return jnp.pad(v, (0, 128 - v.shape[0]))[None, :]

    rate = pad_lanes(-jnp.exp(decay_log))
    bias = pad_lanes(step_bias)
    skip = jnp.repeat(skip_scale, MD)[None, :]
    sgain = state_gain[None, :]

    xs = gather_row(n1)
    xcat, q, raw, sh = kernel(
        proj1_body,
        [((TT, D), BF), ((TT, 128), BF), ((TT, 128), F32), ((TT, 128), BF)],
        (*xs, w_in, pos, cs, sn, kc),
        scal,
        flops=2 * TT * D * 256,
    )
    ps = gather_row(sh)
    z, u, wi, cv = kernel(
        proj2_body,
        [((TT, IW), F32), ((TT, IW), F32), ((TT, 128), F32), ((TT, IW), F32)],
        (xcat, w_in, pos, mixer_kernel, bias),
        flops=2 * TT * D * 774,
    )
    ys = gather_row(dy)
    att, prob, state, send, keep = kernel(
        mixf_body,
        [
            ((TT, 128), BF),
            ((2 * TT, 128), F32),
            ((TT, IW), F32),
            ((2, T, 2176), BF),
            ((2, T, 2176), F32),
        ],
        (q, *ps, pos, z, cv, wi, rate, skip, sgain, w_out),
        scal,
        scratch=(pltpu.VMEM((TT, IW), BF), pltpu.VMEM((TT, 128), F32)),
        flops=2 * TT * 512 * D + 10**9,
    )
    s0, got = scatter_row(send, keep)
    mid, n2, zs, inv2 = kernel(
        mid_body,
        [((T, D), F32), ((T, 1152), BF), ((T, D), F32), ((T, 128), F32)],
        (s0, got, x, gain2),
        mib=16,
    )
    ns = gather_row(n2)
    x2, ycat, isb, hidden, dexp, send, keep = kernel(
        ffn_body,
        [
            ((TT, D), BF),
            ((TT, D), BF),
            ((TT, 128), F32),
            ((TT, HW), BF),
            ((TT, 2 * HW), BF),
            ((2, T, D), BF),
            ((2, T, D), F32),
        ],
        (*ns, *ys, w_ex, w_sh),
        flops=5 * TT * D * D,
    )
    s0, got = scatter_row(send, keep)
    dm, db, g_middle = kernel(
        dmid_body,
        [((T, D), F32), ((T, 1152), BF), ((1, D), F32)],
        (s0, got, mid, inv2, dy, gain2, zs),
        mib=16,
    )
    bs = gather_row(db)
    send, keep = kernel(
        outp_body,
        [((2, T, D), BF), ((2, T, D), F32)],
        (hidden, w_sh),
        flops=2 * TT * HW * D,
        mib=16,
    )
    s0, got = scatter_row(send, keep)
    (out,) = kernel(fin_body, [((T, D), BF)], (s0, got, mid), mib=16)
    outputs = deal_out(out)

    def reduce_col(v):
        return lax.psum_scatter(v.astype(BF), "col", scatter_dimension=0, tiled=True)

    g_shrink = reduce_col(tn(ycat, hidden))
    g_expand = reduce_col(tn(x2, dexp))

    (
        dcat, mixed, dq, dz, du, dw, send, keep, g_mk, g_sgain, g_skip, g_log, g_bias,
    ) = kernel(
        mixb_body,
        [
            ((TT, D), BF),
            ((TT, HW), BF),
            ((TT, 128), BF),
            ((TT, IW), BF),
            ((TT, IW), BF),
            ((TT, 128), BF),
            ((2, TT, 128), BF),
            ((2, TT, 128), F32),
            ((KC, IW), F32),
            ((1, IW), F32),
            ((1, IW), F32),
            ((1, 128), F32),
            ((1, 128), F32),
        ],
        (
            *bs, q, *ps, pos, cs, sn, prob, z, u, cv, state, wi, isb,
            att, rate, skip, sgain, mixer_kernel, w_out,
        ),
        scal,
        scratch=(pltpu.VMEM((TT, HW), F32), pltpu.VMEM((4, T, T), F32)),
        flops=2 * TT * 512 * D + 2 * 10**9,
    )
    recv = xor_row(send, 1)
    s0, s2 = kernel(rss_body, [((TT, 128), F32), ((TT, 128), BF)], (keep, recv), mib=16)
    got = xor_row(s2, 2)
    g_out = reduce_col(tn(dcat, mixed))
    dproj, send, keep, g_kc = kernel(
        dproj_body,
        [((TT, 1030), BF), ((2, T, D), BF), ((2, T, D), F32), ((KC, 128), F32)],
        (s0, got, raw, pos, cs, sn, kc, dq, dz, du, dw, w_in),
        scal,
        flops=2 * TT * D * 1030,
    )
    g_in = reduce_col(tn(xcat, dproj))
    s0, got = scatter_row(send, keep)
    dx, g_input = kernel(
        dx_body, [((T, D), BF), ((1, D), F32)], (s0, got, dm, x, inv1, gain1), mib=16
    )
    input_grad = deal_out(dx)

    def sum_dp(v):
        if groups == 2:
            return v.astype(F32) + lax.ppermute(v, "dp", [(0, 1), (1, 0)]).astype(F32)
        return lax.psum(v, "dp").astype(F32)

    grad_in = sum_dp(g_in)
    grad_out = sum_dp(g_out).T
    grad_expand = sum_dp(g_expand)
    grad_shrink = sum_dp(g_shrink).T

    local = jnp.concatenate(
        [g_mk.reshape(-1), g_sgain.reshape(-1), g_skip.reshape(-1), g_log[0], g_bias[0]]
    )
    span = local.shape[0]
    slots = jnp.where(jnp.arange(SLOTS)[:, None] == r, local[None, :], 0.0).reshape(-1)
    kc_cols = jnp.where(jnp.arange(2)[:, None, None] == (r - 2), g_kc[None], 0.0)
    small = jnp.concatenate([slots, g_input[0], g_middle[0], kc_cols.reshape(-1)])
    small = small.reshape(-1, 128)
    if groups == 2:
        small = small + lax.ppermute(small, "dp", [(0, 1), (1, 0)])
        for k in (1, 2):
            small = small + lax.ppermute(small, "col", [(i, i ^ k) for i in range(4)])
        for k in (1, 2):
            small = small + xor_row(small, k)
    else:
        small = lax.psum(small, ("dp", "row", "col"))
    small = small.reshape(-1)
    local = lax.dynamic_slice_in_dim(small, r * span, span, 0)
    rest = small[SLOTS * span :]
    mine = c * 256
    return (
        outputs,
        input_grad,
        grad_in,
        grad_out,
        grad_expand,
        grad_shrink,
        lax.dynamic_slice_in_dim(rest[0:D], mine, 256, 0),
        lax.dynamic_slice_in_dim(rest[D : 2 * D], mine, 256, 0),
        local[0 : KC * IW].reshape(KC, IW),
        jnp.transpose(rest[2 * D :].reshape(2, KC, 128), (1, 0, 2)).reshape(KC, 256),
        local[KC * IW + 2 * IW : KC * IW + 2 * IW + 6],
        local[KC * IW + 2 * IW + 128 : KC * IW + 2 * IW + 134],
        jnp.sum(local[KC * IW + IW : KC * IW + 2 * IW].reshape(6, MD), axis=1),
        local[KC * IW : KC * IW + IW],
    )


def solution(mesh):
    in_specs = (
        P(("dp", "row"), "col"),
        P(("dp", "row"), "col"),
        P("col", "row"),
        P("row", "col"),
        P("col", "row"),
        P("row", "col"),
        P("col"),
        P("col"),
        P(None, "row"),
        P(),
        P("row"),
        P("row"),
        P("row"),
        P("row"),
        P(),
        P(),
    )
    out_specs = (
        P(("dp", "row"), "col"),
        P(("dp", "row"), "col"),
        P("col", "row"),
        P("row", "col"),
        P("col", "row"),
        P("row", "col"),
        P("col"),
        P("col"),
        P(None, "row"),
        P(),
        P("row"),
        P("row"),
        P("row"),
        P("row"),
    )
    return jax.shard_map(
        per_device, mesh=mesh, in_specs=in_specs, out_specs=out_specs, check_vma=False
    )
```

time: 1640 us -> 390 us (0.24); the launches traced: 1610 us -> 389 us
  blocking collectives: 385 us -> 12.6 us
  matrix products: 246 us -> 10.3 us
  local copies, waits for them, and re-layouts: 299 us -> 77.3 us
  other arithmetic: 140 us -> 9.9 us
  loops' own time: 122 us -> 0 us
  waiting for transfers between devices: 272 us -> 178 us
  starting transfers between devices: 126 us -> 49 us
  Pallas kernels: 0 us -> 34.8 us
    all_gather x32 -> x1, blocking collectives: 288 us -> 12.6 us  [per_device(): lax.all_gather(jnp.stack([input_gain, middle_gain]), 'col', axis=1, tiled...]
    dot_general x156 -> x4, matrix products: 246 us -> 10.3 us  [tn(): lax.dot_general(a, b, (((0,), (0,)), ((), ())), preferred_element_type=F32)]
    another operation x8 -> x0, loops' own time: 122 us -> none  [the longest x4 62.1 us: per_device(): lax.scan(ssd_backward, jnp.zeros((PACK_TOKENS, PACK_TOKENS), jnp.float32)...]
    all_to_all x32 -> x4, starting transfers between devices: 125 us -> 17.5 us  [the longest x2 10.4 us: deal_in(): lax.all_to_all(v.reshape(MB, T, 256), 'col', split_axis=0, concat_axis=0,...]
    all_to_all x32 -> x4, waiting for transfers between devices: 132 us -> 28.7 us  [the longest x2 18.9 us: deal_in(): lax.all_to_all(v.reshape(MB, T, 256), 'col', split_axis=0, concat_axis=0,...]
    psum x7 -> x0, blocking collectives: 96.8 us -> none  [the longest x1 41.5 us: per_device(): lax.psum((lax.dynamic_update_slice(jnp.zeros((D,), jnp.float32), grad_inp...]
    ppermute x0 -> x38, waiting for transfers between devices: none -> 84 us  [the longest x27 60 us: xor_row(): return lax.ppermute(v, 'row', [(i, i ^ k) for i in range(SLOTS)])]
    dynamic_slice x105 -> x4, local copies, waits for them, and re-layouts: 82.5 us -> 2.14 us  [the longest x1 0.86 us: per_device(): lax.dynamic_index_in_dim(lax.dynamic_index_in_dim(dealing, c, 0, False),...]
  transfers between devices with their start and end apart: 53 -> 50, of which waited for: 26 -> 24; matrix products, arithmetic and copies ran while one was open for 40% -> 7% of each run, Pallas kernels for 0% -> 8%
where the time goes in v1:
time: 390 us; the launch traced here: 389 us
  waiting for transfers between devices  178 us (46%)
  local copies, waits for them, and re-layouts  77.3 us (20%)
  starting transfers between devices  49 us (13%)
  Pallas kernels  34.8 us (9%)
  between operations  16.3 us (4%)
  blocking collectives  12.6 us (3%)
  matrix products  10.3 us (3%)
  other arithmetic  9.9 us (3%)
    unnamed x243, local copies, waits for them, and re-layouts  70.8 us
    ppermute x27, waiting for transfers between devices, xor_row(): return lax.ppermute(v, 'row', [(i, i ^ k) for i in range(SLOTS)])  60 us
    all_gather x4, waiting for transfers between devices, gather_col(): return lax.all_gather(v, 'col', axis=0, tiled=True)  36.8 us
    pallas_call x17, Pallas kernels, kernel(): pl.pallas_call(body, out_shape=shapes, in_specs=specs, out_specs=[vm] * l...  34.8 us
    reduce_scatter x4, waiting for transfers between devices, reduce_col(): lax.psum_scatter(v.astype(BF), 'col', scatter_dimension=0, tiled=True)  26.8 us
    all_to_all x2, waiting for transfers between devices, deal_in(): lax.all_to_all(v.reshape(MB, T, 256), 'col', split_axis=0, concat_axis=0,...  18.9 us
    ppermute x2, waiting for transfers between devices, per_device(): small = small + lax.ppermute(small, 'col', [(i, i ^ k) for i in range(4)])  15.6 us
    ppermute x27, starting transfers between devices, xor_row(): return lax.ppermute(v, 'row', [(i, i ^ k) for i in range(SLOTS)])  14.4 us
  transfers between devices with their start and end apart: 50, of which 24 were waited for; matrix products, arithmetic and copies ran while one was open for 7% of the time, Pallas kernels for 8%

profile of v1, /device:TPU:0, one launch (start us, length us, event | category | flops | bytes accessed | tf_op | source)
XLA Modules:
  0.0 388.5 jit_solution(16206622009099910155)
XLA Ops:
  7.3 2.1 copy.54
  10.9 6.3 %all-to-all-start = ((bf16[4,128,256]{2,1,0:T(8,128)(2,1)}), bf16[4,128,256]{2,1,0:T(8,128)(2,1)S(1)}, u32[]{:S(2)}, u32[]{:S(2)}) async-start(bf16[4,128,256]{2,1,0:T(8,128)(2,1)} %bitcast.4), calls=%async_computation | async-start | bytes 524288 | tf_op jit(solution)/shard_map/all_to_all | solution.py:592
  21.1 9.8 %all-to-all-done.own = bf16[4,128,256]{2,1,0:T(8,128)(2,1)S(1)} async-done(((bf16[4,128,256]{2,1,0:T(8,128)(2,1)}), bf16[4,128,256]{2,1,0:T(8,128)(2,1)S(1)}, u32[]{:S(2)}, u32[]{:S(2)}) %all-to-all-start) | async-done | bytes 262176 | tf_op jit(solution)/shard_map/all_to_all | solution.py:592
  30.8 1.6 collective-permute-start
  32.5 12.6 %all_gather.15 = f32[2,1024]{1,0:T(2,128)S(1)} all-gather(f32[2,256]{1,0:T(2,128)S(1)} %pad_maximum_fusion.2), channel_id=1, replica_groups=mesh['dp'=2,'row'=4,'col'=4] {'col'}, dimensions={1}, use_global_device_ids=true | all-gather | bytes 10240 | tf_op jit(solution)/shard_map/all_gather | solution.py:570
  48.1 4.8 %collective-permute-done.2.x2 = bf16[128,1024]{1,0:T(8,128)(2,1)S(1)} collective-permute-done((bf16[128,1024]{1,0:T(8,128)(2,1)S(1)}, bf16[128,1024]{1,0:T(8,128)(2,1)S(1)}, u32[]{:S(2)}, u32[]{:S(2)}) %collective-permute-start.2) | collective-permute-done | bytes 262176 | tf_op jit(solution)/shard_map/ppermute | solution.py:524
  55.8 9.2 %all-gather.5.cloned.1.call-done.w = bf16[1024,1030]{1,0:T(8,128)(2,1)} async-done(((bf16[256,1030]{1,0:T(8,128)(2,1)}), bf16[1024,1030]{1,0:T(8,128)(2,1)}) %all-gather.5.cloned.1.call-update) | async-done | bytes 2109456 | tf_op jit(solution)/shard_map/all_gather | solution.py:564
  65.1 1.7 copy-done.2
  70.6 1.9 shard_map.264
  76.4 4.1 %collective-permute-done.5.p2 = bf16[512,128]{1,0:T(8,128)(2,1)} collective-permute-done((bf16[512,128]{1,0:T(8,128)(2,1)}, bf16[512,128]{1,0:T(8,128)(2,1)}, u32[]{:S(2)}, u32[]{:S(2)}) %collective-permute-start.5) | collective-permute-done | bytes 131104 | tf_op jit(solution)/shard_map/ppermute | solution.py:524
  86.9 6.7 %all-gather.7.cloned.1.call-done = bf16[2048,256]{1,0:T(8,128)(2,1)} async-done(((bf16[512,256]{1,0:T(8,128)(2,1)}), bf16[2048,256]{1,0:T(8,128)(2,1)}) %all-gather.7.cloned.1.call-update) | async-done | bytes 1048592 | tf_op jit(solution)/shard_map/all_gather | solution.py:564
  99.0 5.7 %shard_map.266 = (bf16[512,128]{1,0:T(8,128)(2,1)S(1)}, f32[1024,128]{1,0:T(8,128)S(1)}, f32[512,384]{1,0:T(8,128)S(1)}, bf16[2,128,2176]{2,1,0:T(8,128)(2,1)}, f32[2,128,2176]{2,1,0:T(8,128)S(1)}) custom-call(s32[4]{0:T(128)S(1)} %pad_add_fusion.scal, bf16[512,128]{1,0:T(8,128)(2,1)S(1)} %copy-done.88, bf16[512,128]{1,0:T(8,128)(2,1)} %get-tuple-element.77.p0, ...), custom_call_target="tpu_custom_call" | custom-call | flops 1536870912 | bytes 8588800 | tf_op jit(solution)/shard_map/pallas_call | solution.py:512
  108.4 4.0 %all-to-all-start.1 = ((bf16[4,128,256]{2,1,0:T(8,128)(2,1)}), bf16[4,128,256]{2,1,0:T(8,128)(2,1)}, u32[]{:S(2)}, u32[]{:S(2)}) async-start(bf16[4,128,256]{2,1,0:T(8,128)(2,1)} %bitcast.91), calls=%async_computation.1 | async-start | bytes 524288 | tf_op jit(solution)/shard_map/all_to_all | solution.py:592
  112.7 1.6 copy-done.5
  114.3 2.5 shard_map.267
  119.3 9.1 %all-to-all-done.1 = bf16[4,128,256]{2,1,0:T(8,128)(2,1)} async-done(((bf16[4,128,256]{2,1,0:T(8,128)(2,1)}), bf16[4,128,256]{2,1,0:T(8,128)(2,1)}, u32[]{:S(2)}, u32[]{:S(2)}) %all-to-all-start.1) | async-done | bytes 262176 | tf_op jit(solution)/shard_map/all_to_all | solution.py:592
  129.9 3.3 collective-permute-done.8.recv
  134.5 2.2 shard_map.268
  140.5 7.1 %collective-permute-done.10.n2 = bf16[128,1152]{1,0:T(8,128)(2,1)} collective-permute-done((bf16[128,1152]{1,0:T(8,128)(2,1)}, bf16[128,1152]{1,0:T(8,128)(2,1)}, u32[]{:S(2)}, u32[]{:S(2)}) %collective-permute-start.10) | collective-permute-done | bytes 294944 | tf_op jit(solution)/shard_map/ppermute | solution.py:524
  148.2 3.7 collective-permute-done.14.y2
  154.1 21.0 %all-gather.9.cloned.1.call-done.we = bf16[1024,1024]{1,0:T(8,128)(2,1)} async-done(((bf16[256,1024]{1,0:T(8,128)(2,1)}), bf16[1024,1024]{1,0:T(8,128)(2,1)}) %all-gather.9.cloned.1.call-update) | async-done | bytes 2097168 | tf_op jit(solution)/shard_map/all_gather | solution.py:564
  175.1 1.6 copy-done.62
  180.7 4.3 %shard_map.269 = (bf16[512,1024]{1,0:T(8,128)(2,1)S(1)}, bf16[512,1024]{1,0:T(8,128)(2,1)S(1)}, f32[512,128]{1,0:T(8,128)S(1)}, bf16[512,512]{1,0:T(8,128)(2,1)S...) custom-call(bf16[128,1152]{1,0:T(8,128)(2,1)} %get-tuple-element.87.n0, ...), custom_call_target="tpu_custom_call" | custom-call | flops 2684354560 | bytes 10878976 | tf_op jit(solution)/shard_map/pallas_call | solution.py:512
  189.6 1.7 convolution_convert_fusion.2
  192.3 2.1 collective-permute-done.19.recv
  197.2 6.9 %collective-permute-done.20.recv = bf16[128,1024]{1,0:T(8,128)(2,1)S(1)} collective-permute-done((bf16[128,1024]{1,0:T(8,128)(2,1)S(1)}, bf16[128,1024]{1,0:T(8,128)(2,1)S(1)}, u32[]{:S(2)}, u32[]{:S(2)}) %collective-permute-start.20) | collective-permute-done | bytes 262176 | tf_op jit(solution)/shard_map/ppermute | solution.py:524
  209.1 6.9 %collective-permute-done.22.b2 = bf16[128,1152]{1,0:T(8,128)(2,1)S(1)} collective-permute-done((bf16[128,1152]{1,0:T(8,128)(2,1)S(1)}, bf16[128,1152]{1,0:T(8,128)(2,1)S(1)}, u32[]{:S(2)}, u32[]{:S(2)}) %collective-permute-start.22) | collective-permute-done | bytes 294944 | tf_op jit(solution)/shard_map/ppermute | solution.py:524
  215.9 1.6 collective-permute-done.23.b3
  221.5 9.0 %shard_map.275 = (bf16[512,1024]{1,0:T(8,128)(2,1)S(1)}, bf16[512,512]{1,0:T(8,128)(2,1)S(1)}, bf16[512,128]{1,0:T(8,128)(2,1)S(1)}, bf16[512,384]{1,0:T(8,128)(...) custom-call(s32[4]{0:T(128)S(1)} %pad_add_fusion.scal, ...), custom_call_target="tpu_custom_call" | custom-call | flops 2536870912 | bytes 11423232 | tf_op jit(solution)/shard_map/pallas_call | solution.py:512
  236.3 1.7 convolution_convert_fusion.3
  238.1 4.2 %convolution_convert_fusion.1 = bf16[1024,1024]{1,0:T(8,128)(2,1)} fusion(bf16[512,1024]{1,0:T(8,128)(2,1)} %copy-done.104, bf16[512,1024]{1,0:T(8,128)(2,1)} %copy-done.105), kind=kOutput, calls=%fused_computation.1 | convolution fusion | flops 1074790400 | bytes 4194304 | tf_op jit(solution)/shard_map/dot_general | solution.py:43
  242.8 1.6 collective-permute-done.24.recv
  251.8 2.5 shard_map.277
  256.8 2.7 convolution_convert_fusion
  261.0 1.9 shard_map.271
  264.5 8.1 %collective-permute-done.17.recv = bf16[128,1024]{1,0:T(8,128)(2,1)S(1)} collective-permute-done((bf16[128,1024]{1,0:T(8,128)(2,1)}, bf16[128,1024]{1,0:T(8,128)(2,1)S(1)}, u32[]{:S(2)}, u32[]{:S(2)}) %collective-permute-start.17) | collective-permute-done | bytes 262176 | tf_op jit(solution)/shard_map/ppermute | solution.py:524
  275.5 2.0 collective-permute-done.26.recv
  278.4 7.6 %collective-permute-done.27.recv = bf16[128,1024]{1,0:T(8,128)(2,1)S(1)} collective-permute-done((bf16[128,1024]{1,0:T(8,128)(2,1)S(1)}, bf16[128,1024]{1,0:T(8,128)(2,1)S(1)}, u32[]{:S(2)}, u32[]{:S(2)}) %collective-permute-start.27) | collective-permute-done | bytes 262176 | tf_op jit(solution)/shard_map/ppermute | solution.py:524
  287.8 3.4 all-to-all-start.2
  291.2 2.0 collective-permute-start.34
  294.7 10.2 %collective-permute-done.34 = f32[104,128]{1,0:T(8,128)S(1)} collective-permute-done((f32[104,128]{1,0:T(8,128)S(1)}, f32[104,128]{1,0:T(8,128)S(1)}, u32[]{:S(2)}, u32[]{:S(2)}) %collective-permute-start.34) | collective-permute-done | bytes 53280 | tf_op jit(solution)/shard_map/ppermute | solution.py:786
  304.9 2.7 collective-permute-start.35
  309.1 5.4 %collective-permute-done.35 = f32[104,128]{1,0:T(8,128)S(1)} collective-permute-done((f32[104,128]{1,0:T(8,128)S(1)}, f32[104,128]{1,0:T(8,128)S(1)}, u32[]{:S(2)}, u32[]{:S(2)}) %collective-permute-start.35) | collective-permute-done | bytes 53280 | tf_op jit(solution)/shard_map/ppermute | solution.py:786
  318.3 3.7 all-to-all-start.3
  328.5 9.8 %all-to-all-done.3 = bf16[4,128,256]{2,1,0:T(8,128)(2,1)S(1)} async-done(((bf16[4,128,256]{2,1,0:T(8,128)(2,1)}), bf16[4,128,256]{2,1,0:T(8,128)(2,1)S(1)}, u32[]{:S(2)}, u32[]{:S(2)}) %all-to-all-start.3) | async-done | bytes 262176 | tf_op jit(solution)/shard_map/all_to_all | solution.py:599
  338.4 26.8 %reduce-scatter.5.cloned.1.call-done = bf16[256,1030]{0,1:T(8,128)(2,1)} async-done(((bf16[1024,1030]{0,1:T(8,128)(2,1)}), bf16[256,1030]{0,1:T(8,128)(2,1)}) %reduce-scatter.5.cloned.1.call-update) | async-done | bytes 527376 | tf_op jit(solution)/shard_map/reduce_scatter | solution.py:715
  368.6 2.2 convert_add_fusion.1
  370.8 8.4 %collective-permute-done.29 = bf16[256,1030]{0,1:T(8,128)(2,1)S(1)} collective-permute-done((bf16[256,1030]{0,1:T(8,128)(2,1)}, bf16[256,1030]{0,1:T(8,128)(2,1)S(1)}, u32[]{:S(2)}, u32[]{:S(2)}) %collective-permute-start.29) | collective-permute-done | bytes 527392 | tf_op jit(solution)/shard_map/ppermute | solution.py:767
  (384 shorter events, 110.2 us)
Async XLA Ops:
  7.2 57.8 %all-gather.5.cloned.1.call-start = ((), (), s32[]{:S(2)}) async-start(), calls=%async_computation.8 | async-start | bytes 2949120 | tf_op jit(solution)/shard_map/all_gather | solution.py:564
  9.4 84.2 %all-gather.7.cloned.1.call-start = ((), (), s32[]{:S(2)}) async-start(), calls=%async_computation.9 | async-start | bytes 1310720 | tf_op jit(solution)/shard_map/all_gather | solution.py:564
  10.2 144.0 %all-gather.11.cloned.1.call-start = ((), (), s32[]{:S(2)}) async-start(), calls=%async_computation.11 | async-start | bytes 1310720 | tf_op jit(solution)/shard_map/all_gather | solution.py:564
  10.9 19.9 %all-to-all-start = ((bf16[4,128,256]{2,1,0:T(8,128)(2,1)}), bf16[4,128,256]{2,1,0:T(8,128)(2,1)S(1)}, u32[]{:S(2)}, u32[]{:S(2)}) async-start(bf16[4,128,256]{2,1,0:T(8,128)(2,1)} %bitcast.4), calls=%async_computation | async-start | bytes 524288 | tf_op jit(solution)/shard_map/all_to_all | solution.py:592
  17.2 157.9 %all-gather.9.cloned.1.call-start = ((), (), s32[]{:S(2)}) async-start(), calls=%async_computation.10 | async-start | bytes 2621440 | tf_op jit(solution)/shard_map/all_gather | solution.py:564
  30.8 14.3 %collective-permute-start = (bf16[4,128,256]{2,1,0:T(8,128)(2,1)S(1)}, bf16[4,128,256]{2,1,0:T(8,128)(2,1)S(1)}, u32[]{:S(2)}, u32[]{:S(2)}) collective-permute-start(bf16[4,128,256]{2,1,0:T(8,128)(2,1)S(1)} %all-to-all-done.own), channel_id=1, source_target_pairs={{0,16},{16,0},{1,17},{17,1},{2,18},{18,2},{3,19},{19,3},{4,20},{20... | collective-permute-start | bytes 786440 | tf_op jit(solution)/shard_map/ppermute | solution.py:582
  46.5 6.4 %collective-permute-start.2 = (bf16[128,1024]{1,0:T(8,128)(2,1)S(1)}, bf16[128,1024]{1,0:T(8,128)(2,1)S(1)}, u32[]{:S(2)}, u32[]{:S(2)}) collective-permute-start(bf16[128,1024]{1,0:T(8,128)(2,1)S(1)} %get-tuple-element.75.x0), channel_id=1, source_target_pairs={{0,8},{4,12},{8,0},{12,4},{1,9},{5,13},{9,1},{13,5},{2,10},{6,14},... | collective-permute-start | bytes 786440 | tf_op jit(solution)/shard_map/ppermute | solution.py:524
  48.0 6.4 %collective-permute-start.1 = (bf16[128,1024]{1,0:T(8,128)(2,1)S(1)}, bf16[128,1024]{1,0:T(8,128)(2,1)S(1)}, u32[]{:S(2)}, u32[]{:S(2)}) collective-permute-start(bf16[128,1024]{1,0:T(8,128)(2,1)S(1)} %get-tuple-element.75.x0), channel_id=1, source_target_pairs={{0,4},{4,0},{8,12},{12,8},{1,5},{5,1},{9,13},{13,9},{2,6},{6,2},{1... | collective-permute-start | bytes 786440 | tf_op jit(solution)/shard_map/ppermute | solution.py:524
  52.9 2.2 collective-permute-start.3
  74.8 5.7 %collective-permute-start.5 = (bf16[512,128]{1,0:T(8,128)(2,1)}, bf16[512,128]{1,0:T(8,128)(2,1)}, u32[]{:S(2)}, u32[]{:S(2)}) collective-permute-start(bf16[512,128]{1,0:T(8,128)(2,1)} %get-tuple-element.77.p0), channel_id=1, source_target_pairs={{0,8},{4,12},{8,0},{12,4},{1,9},{5,13},{9,1},{13,5},{2,10},{6,14},... | collective-permute-start | bytes 393224 | tf_op jit(solution)/shard_map/ppermute | solution.py:524
  76.4 17.2 %collective-permute-start.4 = (bf16[512,128]{1,0:T(8,128)(2,1)}, bf16[512,128]{1,0:T(8,128)(2,1)}, u32[]{:S(2)}, u32[]{:S(2)}) collective-permute-start(bf16[512,128]{1,0:T(8,128)(2,1)} %get-tuple-element.77.p0), channel_id=1, source_target_pairs={{0,4},{4,0},{8,12},{12,8},{1,5},{5,1},{9,13},{13,9},{2,6},{6,2},{1... | collective-permute-start | bytes 393224 | tf_op jit(solution)/shard_map/ppermute | solution.py:524
  80.6 13.0 %collective-permute-start.6 = (bf16[512,128]{1,0:T(8,128)(2,1)}, bf16[512,128]{1,0:T(8,128)(2,1)}, u32[]{:S(2)}, u32[]{:S(2)}) collective-permute-start(bf16[512,128]{1,0:T(8,128)(2,1)} %collective-permute-done.5.p2), channel_id=1, source_target_pairs={{0,4},{4,0},{8,12},{12,8},{1,5},{5,1},{9,13},{13,9},{2,6},{6,2},{1... | collective-permute-start | bytes 393224 | tf_op jit(solution)/shard_map/ppermute | solution.py:524
  108.4 4.3 %collective-permute-start.7 = (bf16[2,128,2176]{2,1,0:T(8,128)(2,1)}, bf16[2,128,2176]{2,1,0:T(8,128)(2,1)}, u32[]{:S(2)}, u32[]{:S(2)}) collective-permute-start(bf16[2,128,2176]{2,1,0:T(8,128)(2,1)} %get-tuple-element.83), channel_id=1, source_target_pairs={{0,4},{4,0},{8,12},{12,8},{1,5},{5,1},{9,13},{13,9},{2,6},{6,2},{1... | collective-permute-start | bytes 3342344 | tf_op jit(solution)/shard_map/ppermute | solution.py:524
  108.4 20.0 %all-to-all-start.1 = ((bf16[4,128,256]{2,1,0:T(8,128)(2,1)}), bf16[4,128,256]{2,1,0:T(8,128)(2,1)}, u32[]{:S(2)}, u32[]{:S(2)}) async-start(bf16[4,128,256]{2,1,0:T(8,128)(2,1)} %bitcast.91), calls=%async_computation.1 | async-start | bytes 524288 | tf_op jit(solution)/shard_map/all_to_all | solution.py:592
  112.5 180.8 %reduce-scatter.11.cloned.1.call-start = ((), (), s32[]{:S(2)}) async-start(), calls=%async_computation.15 | async-start | bytes 1310720 | tf_op jit(solution)/shard_map/reduce_scatter | solution.py:715
  117.8 15.4 %collective-permute-start.8 = (bf16[128,2176]{1,0:T(8,128)(2,1)}, bf16[128,2176]{1,0:T(8,128)(2,1)}, u32[]{:S(2)}, u32[]{:S(2)}) collective-permute-start(bf16[128,2176]{1,0:T(8,128)(2,1)} %get-tuple-element.85), channel_id=1, source_target_pairs={{0,8},{4,12},{8,0},{12,4},{1,9},{5,13},{9,1},{13,5},{2,10},{6,14},... | collective-permute-start | bytes 1671176 | tf_op jit(solution)/shard_map/ppermute | solution.py:524
  128.4 10.4 %collective-permute-start.12 = (bf16[4,128,256]{2,1,0:T(8,128)(2,1)}, bf16[4,128,256]{2,1,0:T(8,128)(2,1)}, u32[]{:S(2)}, u32[]{:S(2)}) collective-permute-start(bf16[4,128,256]{2,1,0:T(8,128)(2,1)} %all-to-all-done.1), channel_id=1, source_target_pairs={{0,16},{16,0},{1,17},{17,1},{2,18},{18,2},{3,19},{19,3},{4,20},{20... | collective-permute-start | bytes 786440 | tf_op jit(solution)/shard_map/ppermute | solution.py:582
  137.4 10.2 %collective-permute-start.10 = (bf16[128,1152]{1,0:T(8,128)(2,1)}, bf16[128,1152]{1,0:T(8,128)(2,1)}, u32[]{:S(2)}, u32[]{:S(2)}) collective-permute-start(bf16[128,1152]{1,0:T(8,128)(2,1)} %get-tuple-element.87.n0), channel_id=1, source_target_pairs={{0,8},{4,12},{8,0},{12,4},{1,9},{5,13},{9,1},{13,5},{2,10},{6,14},... | collective-permute-start | bytes 884744 | tf_op jit(solution)/shard_map/ppermute | solution.py:524
  139.9 12.0 %collective-permute-start.14 = (bf16[128,1024]{1,0:T(8,128)(2,1)S(1)}, bf16[128,1024]{1,0:T(8,128)(2,1)S(1)}, u32[]{:S(2)}, u32[]{:S(2)}) collective-permute-start(bf16[128,1024]{1,0:T(8,128)(2,1)S(1)} %bitcast.73), channel_id=1, source_target_pairs={{0,8},{4,12},{8,0},{12,4},{1,9},{5,13},{9,1},{13,5},{2,10},{6,14},... | collective-permute-start | bytes 786440 | tf_op jit(solution)/shard_map/ppermute | solution.py:524
  140.5 34.5 %collective-permute-start.9 = (bf16[128,1152]{1,0:T(8,128)(2,1)}, bf16[128,1152]{1,0:T(8,128)(2,1)}, u32[]{:S(2)}, u32[]{:S(2)}) collective-permute-start(bf16[128,1152]{1,0:T(8,128)(2,1)} %get-tuple-element.87.n0), channel_id=1, source_target_pairs={{0,4},{4,0},{8,12},{12,8},{1,5},{5,1},{9,13},{13,9},{2,6},{6,2},{1... | collective-permute-start | bytes 884744 | tf_op jit(solution)/shard_map/ppermute | solution.py:524
  147.6 27.4 %collective-permute-start.11 = (bf16[128,1152]{1,0:T(8,128)(2,1)}, bf16[128,1152]{1,0:T(8,128)(2,1)}, u32[]{:S(2)}, u32[]{:S(2)}) collective-permute-start(bf16[128,1152]{1,0:T(8,128)(2,1)} %collective-permute-done.10.n2), channel_id=1, source_target_pairs={{0,4},{4,0},{8,12},{12,8},{1,5},{5,1},{9,13},{13,9},{2,6},{6,2},{1... | collective-permute-start | bytes 884744 | tf_op jit(solution)/shard_map/ppermute | solution.py:524
  147.6 4.9 %collective-permute-start.13 = (bf16[128,1024]{1,0:T(8,128)(2,1)S(1)}, bf16[128,1024]{1,0:T(8,128)(2,1)S(1)}, u32[]{:S(2)}, u32[]{:S(2)}) collective-permute-start(bf16[128,1024]{1,0:T(8,128)(2,1)S(1)} %bitcast.74), channel_id=1, source_target_pairs={{0,4},{4,0},{8,12},{12,8},{1,5},{5,1},{9,13},{13,9},{2,6},{6,2},{1... | collective-permute-start | bytes 786440 | tf_op jit(solution)/shard_map/ppermute | solution.py:524
  192.1 131.3 %reduce-scatter.7.cloned.1.call-start = ((), (), s32[]{:S(2)}) async-start(), calls=%async_computation.13 | async-start | bytes 1310720 | tf_op jit(solution)/shard_map/reduce_scatter | solution.py:715
  192.2 2.2 collective-permute-start.19
  195.7 8.4 %collective-permute-start.20 = (bf16[128,1024]{1,0:T(8,128)(2,1)S(1)}, bf16[128,1024]{1,0:T(8,128)(2,1)S(1)}, u32[]{:S(2)}, u32[]{:S(2)}) collective-permute-start(bf16[128,1024]{1,0:T(8,128)(2,1)S(1)} %get-tuple-element.97), channel_id=1, source_target_pairs={{0,8},{4,12},{8,0},{12,4},{1,9},{5,13},{9,1},{13,5},{2,10},{6,14},... | collective-permute-start | bytes 786440 | tf_op jit(solution)/shard_map/ppermute | solution.py:524
  207.6 8.3 %collective-permute-start.22 = (bf16[128,1152]{1,0:T(8,128)(2,1)S(1)}, bf16[128,1152]{1,0:T(8,128)(2,1)S(1)}, u32[]{:S(2)}, u32[]{:S(2)}) collective-permute-start(bf16[128,1152]{1,0:T(8,128)(2,1)S(1)} %get-tuple-element.100.b0), channel_id=1, source_target_pairs={{0,8},{4,12},{8,0},{12,4},{1,9},{5,13},{9,1},{13,5},{2,10},{6,14},... | collective-permute-start | bytes 884744 | tf_op jit(solution)/shard_map/ppermute | solution.py:524
  209.0 6.9 %collective-permute-start.21 = (bf16[128,1152]{1,0:T(8,128)(2,1)S(1)}, bf16[128,1152]{1,0:T(8,128)(2,1)S(1)}, u32[]{:S(2)}, u32[]{:S(2)}) collective-permute-start(bf16[128,1152]{1,0:T(8,128)(2,1)S(1)} %get-tuple-element.100.b0), channel_id=1, source_target_pairs={{0,4},{4,0},{8,12},{12,8},{1,5},{5,1},{9,13},{13,9},{2,6},{6,2},{1... | collective-permute-start | bytes 884744 | tf_op jit(solution)/shard_map/ppermute | solution.py:524
  238.0 86.9 %reduce-scatter.9.cloned.1.call-start = ((), (), s32[]{:S(2)}) async-start(), calls=%async_computation.14 | async-start | bytes 2621440 | tf_op jit(solution)/shard_map/reduce_scatter | solution.py:715
  242.3 122.8 %reduce-scatter.5.cloned.1.call-start = ((), (), s32[]{:S(2)}) async-start(), calls=%async_computation.12 | async-start | bytes 2641920 | tf_op jit(solution)/shard_map/reduce_scatter | solution.py:715
  242.6 1.8 collective-permute-start.24
  245.5 6.3 %collective-permute-start.25 = (bf16[512,128]{1,0:T(8,128)(2,1)S(1)}, bf16[512,128]{1,0:T(8,128)(2,1)S(1)}, u32[]{:S(2)}, u32[]{:S(2)}) collective-permute-start(bf16[512,128]{1,0:T(8,128)(2,1)S(1)} %get-tuple-element.109), channel_id=1, source_target_pairs={{0,8},{4,12},{8,0},{12,4},{1,9},{5,13},{9,1},{13,5},{2,10},{6,14},... | collective-permute-start | bytes 393224 | tf_op jit(solution)/shard_map/ppermute | solution.py:524
  251.8 7.8 %collective-permute-start.16 = (bf16[2,128,1024]{2,1,0:T(8,128)(2,1)}, bf16[2,128,1024]{2,1,0:T(8,128)(2,1)}, u32[]{:S(2)}, u32[]{:S(2)}) collective-permute-start(bf16[2,128,1024]{2,1,0:T(8,128)(2,1)} %get-tuple-element.90), channel_id=1, source_target_pairs={{0,4},{4,0},{8,12},{12,8},{1,5},{5,1},{9,13},{13,9},{2,6},{6,2},{1... | collective-permute-start | bytes 1572872 | tf_op jit(solution)/shard_map/ppermute | solution.py:524
  263.7 8.9 %collective-permute-start.17 = (bf16[128,1024]{1,0:T(8,128)(2,1)}, bf16[128,1024]{1,0:T(8,128)(2,1)S(1)}, u32[]{:S(2)}, u32[]{:S(2)}) collective-permute-start(bf16[128,1024]{1,0:T(8,128)(2,1)} %get-tuple-element.92), channel_id=1, source_target_pairs={{0,8},{4,12},{8,0},{12,4},{1,9},{5,13},{9,1},{13,5},{2,10},{6,14},... | collective-permute-start | bytes 786440 | tf_op jit(solution)/shard_map/ppermute | solution.py:524
  273.7 13.3 %collective-permute-start.18 = (bf16[128,1024]{1,0:T(8,128)(2,1)S(1)}, bf16[128,1024]{1,0:T(8,128)(2,1)S(1)}, u32[]{:S(2)}, u32[]{:S(2)}) collective-permute-start(bf16[128,1024]{1,0:T(8,128)(2,1)S(1)} %shard_map.272), channel_id=1, source_target_pairs={{0,16},{16,0},{1,17},{17,1},{2,18},{18,2},{3,19},{19,3},{4,20},{20... | collective-permute-start | bytes 786440 | tf_op jit(solution)/shard_map/ppermute | solution.py:582
  275.3 2.2 collective-permute-start.26
  277.6 8.4 %collective-permute-start.27 = (bf16[128,1024]{1,0:T(8,128)(2,1)S(1)}, bf16[128,1024]{1,0:T(8,128)(2,1)S(1)}, u32[]{:S(2)}, u32[]{:S(2)}) collective-permute-start(bf16[128,1024]{1,0:T(8,128)(2,1)S(1)} %get-tuple-element.118), channel_id=1, source_target_pairs={{0,8},{4,12},{8,0},{12,4},{1,9},{5,13},{9,1},{13,5},{2,10},{6,14},... | collective-permute-start | bytes 786440 | tf_op jit(solution)/shard_map/ppermute | solution.py:524
  286.4 4.8 %collective-permute-start.33 = (f32[104,128]{1,0:T(8,128)S(1)}, f32[104,128]{1,0:T(8,128)S(1)}, u32[]{:S(2)}, u32[]{:S(2)}) collective-permute-start(f32[104,128]{1,0:T(8,128)S(1)} %maximum_bitcast_fusion), channel_id=1, source_target_pairs={{0,16},{16,0},{1,17},{17,1},{2,18},{18,2},{3,19},{19,3},{4,20},{20... | collective-permute-start | bytes 159752 | tf_op jit(solution)/shard_map/ppermute | solution.py:784
  287.8 21.3 %all-to-all-start.2 = ((bf16[4,128,256]{2,1,0:T(8,128)(2,1)}), bf16[4,128,256]{2,1,0:T(8,128)(2,1)S(1)}, u32[]{:S(2)}, u32[]{:S(2)}) async-start(bf16[4,128,256]{2,1,0:T(8,128)(2,1)} %bitcast.72), calls=%async_computation.2 | async-start | bytes 524288 | tf_op jit(solution)/shard_map/all_to_all | solution.py:599
  291.2 13.7 %collective-permute-start.34 = (f32[104,128]{1,0:T(8,128)S(1)}, f32[104,128]{1,0:T(8,128)S(1)}, u32[]{:S(2)}, u32[]{:S(2)}) collective-permute-start(f32[104,128]{1,0:T(8,128)S(1)} %fusion.3), channel_id=1, source_target_pairs={{0,1},{1,0},{2,3},{3,2},{4,5},{5,4},{6,7},{7,6},{8,9},{9,8},{10,11... | collective-permute-start | bytes 159752 | tf_op jit(solution)/shard_map/ppermute | solution.py:786
  293.3 21.3 %collective-permute-start.32 = (bf16[256,512]{1,0:T(8,128)(2,1)}, bf16[256,512]{1,0:T(8,128)(2,1)S(1)}, u32[]{:S(2)}, u32[]{:S(2)}) collective-permute-start(bf16[256,512]{1,0:T(8,128)(2,1)} %reduce-scatter.11.cloned.1.call-done), channel_id=1, source_target_pairs={{0,16},{16,0},{1,17},{17,1},{2,18},{18,2},{3,19},{19,3},{4,20},{20... | collective-permute-start | bytes 786440 | tf_op jit(solution)/shard_map/ppermute | solution.py:767
  304.9 9.6 %collective-permute-start.35 = (f32[104,128]{1,0:T(8,128)S(1)}, f32[104,128]{1,0:T(8,128)S(1)}, u32[]{:S(2)}, u32[]{:S(2)}) collective-permute-start(f32[104,128]{1,0:T(8,128)S(1)} %fusion.16), channel_id=1, source_target_pairs={{0,2},{1,3},{2,0},{3,1},{4,6},{5,7},{6,4},{7,5},{8,10},{9,11},{10,... | collective-permute-start | bytes 159752 | tf_op jit(solution)/shard_map/ppermute | solution.py:786
  307.7 9.9 %collective-permute-start.28 = (bf16[128,1024]{1,0:T(8,128)(2,1)S(1)}, bf16[128,1024]{1,0:T(8,128)(2,1)S(1)}, u32[]{:S(2)}, u32[]{:S(2)}) collective-permute-start(bf16[128,1024]{1,0:T(8,128)(2,1)S(1)} %get-tuple-element.121), channel_id=1, source_target_pairs={{0,16},{16,0},{1,17},{17,1},{2,18},{18,2},{3,19},{19,3},{4,20},{20... | collective-permute-start | bytes 786440 | tf_op jit(solution)/shard_map/ppermute | solution.py:582
  314.5 2.1 collective-permute-start.36
  316.7 5.3 %collective-permute-start.37 = (f32[104,128]{1,0:T(8,128)S(1)}, f32[104,128]{1,0:T(8,128)S(1)}, u32[]{:S(2)}, u32[]{:S(2)}) collective-permute-start(f32[104,128]{1,0:T(8,128)S(1)} %add.82), channel_id=1, source_target_pairs={{0,8},{4,12},{8,0},{12,4},{1,9},{5,13},{9,1},{13,5},{2,10},{6,14},... | collective-permute-start | bytes 159752 | tf_op jit(solution)/shard_map/ppermute | solution.py:524
  318.3 20.1 %all-to-all-start.3 = ((bf16[4,128,256]{2,1,0:T(8,128)(2,1)}), bf16[4,128,256]{2,1,0:T(8,128)(2,1)S(1)}, u32[]{:S(2)}, u32[]{:S(2)}) async-start(bf16[4,128,256]{2,1,0:T(8,128)(2,1)} %bitcast.70), calls=%async_computation.3 | async-start | bytes 524288 | tf_op jit(solution)/shard_map/all_to_all | solution.py:599
  323.4 43.2 %collective-permute-start.30 = (bf16[256,512]{1,0:T(8,128)(2,1)}, bf16[256,512]{1,0:T(8,128)(2,1)S(1)}, u32[]{:S(2)}, u32[]{:S(2)}) collective-permute-start(bf16[256,512]{1,0:T(8,128)(2,1)} %reduce-scatter.7.cloned.1.call-done), channel_id=1, source_target_pairs={{0,16},{16,0},{1,17},{17,1},{2,18},{18,2},{3,19},{19,3},{4,20},{20... | collective-permute-start | bytes 786440 | tf_op jit(solution)/shard_map/ppermute | solution.py:767
  324.9 43.7 %collective-permute-start.31 = (bf16[256,1024]{1,0:T(8,128)(2,1)}, bf16[256,1024]{1,0:T(8,128)(2,1)}, u32[]{:S(2)}, u32[]{:S(2)}) collective-permute-start(bf16[256,1024]{1,0:T(8,128)(2,1)} %reduce-scatter.9.cloned.1.call-done), channel_id=1, source_target_pairs={{0,16},{16,0},{1,17},{17,1},{2,18},{18,2},{3,19},{19,3},{4,20},{20... | collective-permute-start | bytes 1572872 | tf_op jit(solution)/shard_map/ppermute | solution.py:767
  365.1 14.1 %collective-permute-start.29 = (bf16[256,1030]{0,1:T(8,128)(2,1)}, bf16[256,1030]{0,1:T(8,128)(2,1)S(1)}, u32[]{:S(2)}, u32[]{:S(2)}) collective-permute-start(bf16[256,1030]{0,1:T(8,128)(2,1)} %reduce-scatter.5.cloned.1.call-done), channel_id=1, source_target_pairs={{0,16},{16,0},{1,17},{17,1},{2,18},{18,2},{3,19},{19,3},{4,20},{20... | collective-permute-start | bytes 1582088 | tf_op jit(solution)/shard_map/ppermute | solution.py:767
  (119 other events, 910.9 us)
Sparse Core Ops, SparseCore 0:
  10.2 54.7 all-gather.4
  66.6 26.9 all-gather.6
  95.2 33.5 all-gather.10
  130.2 44.7 all-gather.8
  192.2 25.8 reduce-scatter.10
  238.1 25.8 reduce-scatter.6
  266.3 48.9 reduce-scatter.8
  317.7 47.3 reduce-scatter.4
